TPU v7x, 32 devices: a whole 2x2x4 slice. The times are simulated.
32 devices in a mesh: band: 8 (over z, y), mp: 4 (over x, core).
Axes of the slice: x: 2, y: 2, z: 4, core: 2. Of those that a mesh axis runs over, the one named last changes fastest.
Arguments:
- node_adjoint: bfloat16 [8192, 512], P('band'), may hold values from -6 to 6
- band_map: int32 [8, 1024], P('band'), may hold values from 0 to 1023, each once within a row
- latents: bfloat16 [8192, 512], P('band'), may hold values from -20 to 20
- observations: bfloat16 [4096, 512], P('band'), may hold values from -6 to 6
- route_band: int32 [4096, 1], P('band'), may hold values from 0 to 7; in each aligned block of 512 rows (0 to 511, 512 to 1023, ...) at most 128 rows name the same one
- route_cell: int32 [4096], P('band'), may hold values from 0 to 1023
- block_mask: int32 [64, 8], P('band'), may hold values 0 or 1
- w_query: bfloat16 [512, 512], P(None, 'mp'), may hold values from -2 to 2
- w_key: bfloat16 [512, 512], P(None, 'mp'), may hold values from -2 to 2
- w_value: bfloat16 [512, 512], P(None, 'mp'), may hold values from -0.25 to 0.25
- w_out: bfloat16 [512, 512], P('mp'), may hold values from -0.25 to 0.25
Outputs:
- node_grad: bfloat16 [8192, 512], P('band', 'mp')
- observation_grad: bfloat16 [4096, 512], P('band', 'mp')
Inputs may be any that keep to these rules, and one draw needn't show every extreme that they name: Row q places the 1024 nodes of band q in the processor's partitions: node n of band q is row q * 128 + band_map[q, n] % 128 of partition band_map[q, n] // 128; each row holds every value once. `route_band`: within the rows of one device no band is named by more than 128 rows, a bound that some block reaches.
All inputs are finite; a program needn't handle non-finite values. No bound on the sum of `block_mask` on one device may be relied on, other than what follows from the above.
Results may differ from a plain program's by a relative error of at most 0.012.
The roundings to bfloat16 on the way count: a program that leaves them out, or rounds other values in their place, can miss the bound.
Values may be sent and summed in bfloat16 or wider, within the bound.
A program may use at most 64 MiB of HBM per device.

v0:
```python
import math

import jax
import jax.numpy as jnp
from jax import lax
from jax.sharding import PartitionSpec as P

HEAD_DIM = 32
BLOCK = 128


def dot_wide(left, right):
    return jnp.dot(left, right, preferred_element_type=jnp.float32)


def dot_transposed(left, right):
    return lax.dot_general(
        left, right, (((1,), (1,)), ((), ())), preferred_element_type=jnp.float32
    )


def broaden_precision(value):
    return lax.optimization_barrier(value).astype(jnp.float32)


def send_slots(route_band, band_count, capacity):
    target = route_band[:, 0]
    onehot = (target[:, None] == jnp.arange(band_count, dtype=jnp.int32)[None, :]).astype(jnp.int32)
    earlier = jnp.cumsum(onehot, axis=0) - onehot
    rank_within = jnp.sum(earlier * onehot, axis=1)
    return target * capacity + rank_within


def on_device(
    node_adjoint,
    band_map,
    latents,
    observations,
    route_band,
    route_cell,
    block_mask,
    w_query,
    w_key,
    w_value,
    w_out,
):
    band_count = lax.axis_size("band")
    node_count = latents.shape[0]
    column_count = w_query.shape[1]
    head_count = column_count // HEAD_DIM
    observed_rows = observations.shape[0]
    capacity = 2 * observed_rows // band_count
    slot_count = capacity * band_count
    block_count = block_mask.shape[1]
    model_index = lax.axis_index("mp")
    score_factor_scale = 1.0 / math.sqrt(HEAD_DIM)
    w_pair = jnp.concatenate([w_key, w_value], axis=1)
    arrival = band_map[0]
    received = lax.all_to_all(node_adjoint, "band", split_axis=0, concat_axis=0, tiled=True)
    adjoint = jnp.take(received, arrival, axis=0)
    adjoint_part = lax.dynamic_slice_in_dim(adjoint, model_index * column_count, column_count, 1)
    target_slot = send_slots(route_band, band_count, capacity)
    cell_send = jnp.full((slot_count,), -1, jnp.int32).at[target_slot].set(route_cell)
    own_rows = lax.dynamic_slice_in_dim(observations, model_index * column_count, column_count, 1)
    row_send = jnp.zeros((slot_count, column_count), jnp.bfloat16).at[target_slot].set(own_rows)
    row_arrived, slot_cells = (
        lax.all_to_all(row_send, "band", split_axis=0, concat_axis=0, tiled=True),
        lax.all_to_all(cell_send, "band", split_axis=0, concat_axis=0, tiled=True),
    )
    full_rows = lax.all_gather(row_arrived, "mp", axis=1, tiled=True)
    key_pairs = dot_wide(full_rows, w_pair).astype(jnp.bfloat16)
    key_head_split = key_pairs[:, :column_count].reshape(slot_count, head_count, HEAD_DIM)
    value_heads = key_pairs[:, column_count:].reshape(slot_count, head_count, HEAD_DIM)
    key_hot = (
        (slot_cells // BLOCK)[:, None] == jnp.arange(block_count, dtype=jnp.int32)[None, :]
    ).astype(jnp.bfloat16)
    node_mask = jnp.repeat(block_mask, BLOCK, axis=0).astype(jnp.bfloat16)
    queries = (dot_wide(latents, w_query) * score_factor_scale).astype(jnp.bfloat16)
    self_pair = dot_wide(latents, w_pair).astype(jnp.bfloat16)
    self_pair_key = self_pair[:, :column_count]
    self_value = self_pair[:, column_count:]
    grad_out = dot_transposed(adjoint, w_out).astype(jnp.bfloat16)
    block_rows = min(512, node_count)
    block_total = node_count // block_rows

    def split_blocks(value):
        return value.reshape(block_total, block_rows, head_count, HEAD_DIM)

    stacked = (
        split_blocks(queries),
        split_blocks(self_pair_key),
        split_blocks(self_value),
        split_blocks(grad_out),
        node_mask.reshape(block_total, block_rows, block_count),
    )

    def attend(running, block_entries):
        key_grad, value_grad = running
        query_tile, self_key_tile, self_value_tile, gradient_block, block_mask_tile = block_entries
        scores = jnp.einsum(
            "qhd,khd->hqk", query_tile, key_head_split, preferred_element_type=jnp.float32
        )
        allowed = (dot_transposed(block_mask_tile, key_hot) > 0.5)[None]
        query_widened = broaden_precision(query_tile)
        grad_wide = broaden_precision(gradient_block)
        self_key_widened = broaden_precision(self_key_tile)
        self_score = jnp.transpose(jnp.sum(query_widened * self_key_widened, axis=2))
        highest = jnp.maximum(jnp.max(jnp.where(allowed, scores, -jnp.inf), axis=2), self_score)
        weights = jnp.where(allowed, jnp.exp(scores - highest[:, :, None]), 0.0)
        own_weight = jnp.exp(self_score - highest)
        normaliser = jnp.sum(weights, axis=2) + own_weight
        probabilities = weights / normaliser[:, :, None]
        own_prob = own_weight / normaliser
        probabilities_low = probabilities.astype(jnp.bfloat16)
        dprobs = jnp.einsum(
            "qhd,khd->hqk", gradient_block, value_heads, preferred_element_type=jnp.float32
        )
        own_dprob = jnp.transpose(jnp.sum(grad_wide * broaden_precision(self_value_tile), axis=2))
        centre = jnp.sum(probabilities * dprobs, axis=2) + own_prob * own_dprob
        dscore = probabilities * (dprobs - centre[:, :, None])
        own_dscore = own_prob * (own_dprob - centre)
        score_gradient_narrow = dscore.astype(jnp.bfloat16)
        self_score_gradient_rows = jnp.transpose(own_dscore)[:, :, None]
        own_prob_rows = jnp.transpose(own_prob)[:, :, None]
        query_gradient = jnp.einsum(
            "hqk,khd->qhd",
            score_gradient_narrow,
            key_head_split,
            preferred_element_type=jnp.float32,
        )
        query_gradient = (
            (query_gradient + self_score_gradient_rows * self_key_widened) * score_factor_scale
        ).astype(jnp.bfloat16)
        dself_key = (self_score_gradient_rows * query_widened).astype(jnp.bfloat16)
        dself_value = (own_prob_rows * grad_wide).astype(jnp.bfloat16)
        key_grad = key_grad + jnp.einsum(
            "hqk,qhd->khd", score_gradient_narrow, query_tile, preferred_element_type=jnp.float32
        )
        value_grad = value_grad + jnp.einsum(
            "hqk,qhd->khd", probabilities_low, gradient_block, preferred_element_type=jnp.float32
        )
        flat_shape = (block_rows, column_count)
        node_pieces = jnp.concatenate(
            [
                query_gradient.reshape(flat_shape),
                dself_key.reshape(flat_shape),
                dself_value.reshape(flat_shape),
            ],
            axis=1,
        )
        return ((key_grad, value_grad), node_pieces)

    zero_grads = jnp.zeros((slot_count, head_count, HEAD_DIM), jnp.float32)
    (key_grad, value_grad), node_pieces = lax.scan(attend, (zero_grads, zero_grads), stacked)
    node_pieces = node_pieces.reshape(node_count, 3 * column_count)
    w_triple = jnp.concatenate([w_query, w_key, w_value], axis=1)
    node_term = dot_transposed(node_pieces, w_triple)
    node_sum = lax.psum_scatter(
        node_term.astype(jnp.bfloat16), "mp", scatter_dimension=1, tiled=True
    ).astype(jnp.float32)
    node_grad = (adjoint_part.astype(jnp.float32) + node_sum).astype(jnp.bfloat16)
    grad_pairs = jnp.concatenate(
        [
            key_grad.astype(jnp.bfloat16).reshape(slot_count, column_count),
            value_grad.astype(jnp.bfloat16).reshape(slot_count, column_count),
        ],
        axis=1,
    )
    slot_term = dot_transposed(grad_pairs, w_pair)
    slot_sum = lax.psum_scatter(
        slot_term.astype(jnp.bfloat16), "mp", scatter_dimension=1, tiled=True
    )
    returned = lax.all_to_all(slot_sum, "band", split_axis=0, concat_axis=0, tiled=True)
    observation_grad = jnp.take(returned, target_slot, axis=0)
    return (node_grad, observation_grad)


def solution(mesh):
    return jax.shard_map(
        on_device,
        mesh=mesh,
        in_specs=(
            P("band", None),
            P("band", None),
            P("band", None),
            P("band", None),
            P("band", None),
            P("band"),
            P("band", None),
            P(None, "mp"),
            P(None, "mp"),
            P(None, "mp"),
            P("mp", None),
        ),
        out_specs=(P("band", "mp"), P("band", "mp")),
        check_vma=False,
    )
```

profile of v0, /device:TPU:0, one launch (start us, length us, event | category | flops | bytes accessed | tf_op | source)
XLA Modules:
  0.0 192.9 jit_solution(368818588823533489)
XLA Ops:
  11.4 3.2 %scatter_custom_fusion = s32[1024]{0:T(1024)} fusion(s32[512]{0:T(512)S(1)} %bitcast.197, s32[512]{0:T(512)} %param.18, s32[]{:T(128)} %constant.84.clone.1), kind=kCustom, calls=%fused_computation.100 | custom fusion | bytes 4608 | tf_op jit(solution)/shard_map/scatter | solution.py:63
  14.5 7.3 %all-to-all-start.1 = ((s32[8,128,1]{1,2,0:T(1,128)}), s32[8,128,1]{1,2,0:T(1,128)S(1)}, u32[]{:S(2)}, u32[]{:S(2)}) async-start(s32[8,128,1]{1,2,0:T(1,128)} %bitcast.18), calls=%async_computation.1 | async-start | bytes 8192 | tf_op jit(solution)/shard_map/all_to_all | solution.py:68
  21.9 2.2 %scatter_custom_fusion.1 = bf16[1024,128]{1,0:T(8,128)(2,1)S(1)} fusion(s32[512]{0:T(512)S(1)} %bitcast.198, bf16[512,512]{1,0:T(8,128)(2,1)} %param.16, s32[]{:T(128)} %constant.74.clone.1, s32[]{:T(128)S(6)} %select_n.55, bf16[]{:T(256)} %constant.82.clone.1), kind=kCustom, calls=%fused_computation.73 | custom fusion | bytes 394244 | tf_op jit(solution)/shard_map/scatter | solution.py:65
  24.0 4.2 %all-to-all-done.1 = s32[8,128,1]{1,2,0:T(1,128)S(1)} async-done(((s32[8,128,1]{1,2,0:T(1,128)}), s32[8,128,1]{1,2,0:T(1,128)S(1)}, u32[]{:S(2)}, u32[]{:S(2)}) %all-to-all-start.1) | async-done | bytes 4128 | tf_op jit(solution)/shard_map/all_to_all | solution.py:68
  28.3 11.3 %all_to_all.48 = bf16[8,128,128]{2,1,0:T(8,128)(2,1)} all-to-all(bf16[8,128,128]{2,1,0:T(8,128)(2,1)S(1)} %bitcast.188), channel_id=1, replica_groups=mesh['band'=8,'mp'=4] {'band'}, dimensions={0} | all-to-all | bytes 524288 | tf_op jit(solution)/shard_map/all_to_all | solution.py:67
  39.5 3.6 %all-to-all-start = ((bf16[8,128,512]{2,1,0:T(8,128)(2,1)}), bf16[8,128,512]{2,1,0:T(8,128)(2,1)S(1)}, u32[]{:S(2)}, u32[]{:S(2)}) async-start(bf16[8,128,512]{2,1,0:T(8,128)(2,1)} %bitcast.186), calls=%async_computation | async-start | bytes 2097152 | tf_op jit(solution)/shard_map/all_to_all | solution.py:59
  47.7 1.8 reshape.148
  50.6 2.0 %fusion.34 = bf16[1024,128]{1,0:T(8,128)(2,1)} fusion(bf16[1024,512]{1,0:T(8,128)(2,1)S(1)} %copy-done, bf16[512,128]{1,0:T(8,128)(2,1)} %param.20), kind=kOutput, calls=%fused_computation.61 | convolution fusion | flops 134479872 | bytes 1441792 | tf_op jit(solution)/shard_map/dot_general | solution.py:13
  52.6 1.8 copy.24
  54.4 1.9 reshape.142
  56.3 1.7 copy.27
  58.6 8.5 %all-to-all-done = bf16[8,128,512]{2,1,0:T(8,128)(2,1)S(1)} async-done(((bf16[8,128,512]{2,1,0:T(8,128)(2,1)}), bf16[8,128,512]{2,1,0:T(8,128)(2,1)S(1)}, u32[]{:S(2)}, u32[]{:S(2)}) %all-to-all-start) | async-done | bytes 1048608 | tf_op jit(solution)/shard_map/all_to_all | solution.py:59
  67.1 5.1 %gather_fusion = bf16[1024,512]{1,0:T(8,128)(2,1)} fusion(bf16[1024,512]{1,0:T(8,128)(2,1)S(1)} %bitcast.176, s32[1024]{0:T(1024)S(1)} %broadcast_clamp_fusion), kind=kCustom, calls=%fused_computation | custom fusion | bytes 2101248 | tf_op jit(solution)/shard_map/jit(_take)/gather | solution.py:60
  75.5 1.7 convolution_convert_fusion.3
  78.7 47.6 %while.15 = (s32[]{:T(128)}, f32[1024,4,32]{0,2,1:T(8,128)S(1)}, f32[1024,4,32]{0,2,1:T(8,128)}, bf16[2,512,384]{2,1,0:T(8,128)(2,1)}, bf16[2,512,4,32]{1,3,2,0:...) while((s32[]{:T(128)}, f32[1024,4,32]{0,2,1:T(8,128)S(1)}, ...), condition=%wide.region_11.12_spmd.clone, body=%wide.region_5.11_spmd.clone.sunk | while | flops 724936704 | bytes 157332928 | solution.py:154
  82.6 2.5 %fusion.112 = f32[4,512]{1,0:T(4,128)S(1)} fusion(f32[4,512,1024]{2,1,0:T(8,128)S(1)} %get-tuple-element.271, f32[4,512]{1,0:T(4,128)S(1)} %bitcast_maximum_fusion.2, pred[512,1024]{1,0:T(8,128)(4,1)S(1)} %convolution_compare_fusion.2), kind=kLoop, calls=%fused_computation.10.clone.1 | loop fusion | flops 6289408 | bytes 8929280 | tf_op jit(solution)/shard_map/while/body/eval_jaxpr/reduce_sum | solution.py:111
  85.2 3.3 %multiply_reduce_fusion.2 = (f32[4,512]{1,0:T(4,128)S(1)}, f32[4,512,1024]{2,1,0:T(8,128)S(1)}) fusion(f32[4,512]{1,0:T(4,128)S(1)} %fusion.113, f32[4,512,1024]{2,1,0:T(8,128)S(1)} %get-tuple-element.271, f32[4,512]{1,0:T(4,128)S(1)} %bitcast_maximum_fusion.2, pred[512,1024]{1,0:T(8,128)(4,1)S(1)} %convolution_compare_fusion.2, ...), kind=kOutput, calls=%fused_computation.6.clone.1 | convolution fusion | flops 144701440 | bytes 17719296 | tf_op jit(solution)/shard_map/while/body/eval_jaxpr/qhd,khd->hqk/dot_general | solution.py:115
  88.6 2.7 %multiply_convert_fusion.2 = bf16[4,512,1024]{2,1,0:T(8,128)(2,1)S(1)} fusion(f32[4,512,1024]{2,1,0:T(8,128)S(1)} %get-tuple-element.275, f32[4,512]{1,0:T(4,128)S(1)} %fusion.115, f32[4,512]{1,0:T(4,128)S(1)} %fusion.113, f32[4,512,1024]{2,1,0:T(8,128)S(1)} %get-tuple-element.271, f32[4,512]{1,0:T(4,128)S(1)} %bitcast_maximum_fusion.2, ...), kind=kLoop, calls=%fused_computation.5.clone.1 | loop fusion | flops 12582912 | bytes 21520384 | tf_op jit(solution)/shard_map/while/body/eval_jaxpr/convert_element_type | solution.py:122
  91.3 1.9 %copy-done.2 = bf16[4,512,1024]{2,1,0:T(8,128)(2,1)} copy-done((bf16[4,512,1024]{2,1,0:T(8,128)(2,1)}, bf16[4,512,1024]{2,1,0:T(8,128)(2,1)S(1)}, u32[]{:S(2)}) %copy-start.2) | copy-done | bytes 4194328 | tf_op jit(solution)/shard_map/while
  95.7 5.7 %fusion.117 = f32[1024,4,32]{0,2,1:T(8,128)} fusion(bf16[512,4,32]{0,2,1:T(8,128)(2,1)S(1)} %get-tuple-element.274, f32[1024,4,32]{0,2,1:T(8,128)} %get-tuple-element.296, pred[]{:T(512)S(6)} %compare.10, f32[4,512,1024]{2,1,0:T(8,128)} %copy-done.1, f32[4,512]{1,0:T(4,128)S(1)} %fusion.113, f32[4,512]{1,0:T(4,128)S(1)} %bitcast_maximum_fusion.2, ...), kind=kOutput, calls=%fused_computation.17.clone.1 | convolution fusion | flops 142868480 | bytes 10108929 | tf_op jit(solution)/shard_map/while/body/eval_jaxpr/hqk,qhd->khd/dot_general | solution.py:139
  104.8 1.5 select_reduce_fusion.2
  106.4 2.5 %fusion.112 = f32[4,512]{1,0:T(4,128)S(1)} fusion(f32[4,512,1024]{2,1,0:T(8,128)S(1)} %get-tuple-element.271, f32[4,512]{1,0:T(4,128)S(1)} %bitcast_maximum_fusion.2, pred[512,1024]{1,0:T(8,128)(4,1)S(1)} %convolution_compare_fusion.2), kind=kLoop, calls=%fused_computation.10.clone.1 | loop fusion | flops 6289408 | bytes 8929280 | tf_op jit(solution)/shard_map/while/body/eval_jaxpr/reduce_sum | solution.py:111
  109.0 3.3 %multiply_reduce_fusion.2 = (f32[4,512]{1,0:T(4,128)S(1)}, f32[4,512,1024]{2,1,0:T(8,128)S(1)}) fusion(f32[4,512]{1,0:T(4,128)S(1)} %fusion.113, f32[4,512,1024]{2,1,0:T(8,128)S(1)} %get-tuple-element.271, f32[4,512]{1,0:T(4,128)S(1)} %bitcast_maximum_fusion.2, pred[512,1024]{1,0:T(8,128)(4,1)S(1)} %convolution_compare_fusion.2, ...), kind=kOutput, calls=%fused_computation.6.clone.1 | convolution fusion | flops 144701440 | bytes 17719296 | tf_op jit(solution)/shard_map/while/body/eval_jaxpr/qhd,khd->hqk/dot_general | solution.py:115
  112.4 2.7 %multiply_convert_fusion.2 = bf16[4,512,1024]{2,1,0:T(8,128)(2,1)S(1)} fusion(f32[4,512,1024]{2,1,0:T(8,128)S(1)} %get-tuple-element.275, f32[4,512]{1,0:T(4,128)S(1)} %fusion.115, f32[4,512]{1,0:T(4,128)S(1)} %fusion.113, f32[4,512,1024]{2,1,0:T(8,128)S(1)} %get-tuple-element.271, f32[4,512]{1,0:T(4,128)S(1)} %bitcast_maximum_fusion.2, ...), kind=kLoop, calls=%fused_computation.5.clone.1 | loop fusion | flops 12582912 | bytes 21520384 | tf_op jit(solution)/shard_map/while/body/eval_jaxpr/convert_element_type | solution.py:122
  115.1 1.9 %copy-done.2 = bf16[4,512,1024]{2,1,0:T(8,128)(2,1)} copy-done((bf16[4,512,1024]{2,1,0:T(8,128)(2,1)}, bf16[4,512,1024]{2,1,0:T(8,128)(2,1)S(1)}, u32[]{:S(2)}) %copy-start.2) | copy-done | bytes 4194328 | tf_op jit(solution)/shard_map/while
  119.5 5.9 %fusion.117 = f32[1024,4,32]{0,2,1:T(8,128)} fusion(bf16[512,4,32]{0,2,1:T(8,128)(2,1)S(1)} %get-tuple-element.274, f32[1024,4,32]{0,2,1:T(8,128)} %get-tuple-element.296, pred[]{:T(512)S(6)} %compare.10, f32[4,512,1024]{2,1,0:T(8,128)} %copy-done.1, f32[4,512]{1,0:T(4,128)S(1)} %fusion.113, f32[4,512]{1,0:T(4,128)S(1)} %bitcast_maximum_fusion.2, ...), kind=kOutput, calls=%fused_computation.17.clone.1 | convolution fusion | flops 142868480 | bytes 10108929 | tf_op jit(solution)/shard_map/while/body/eval_jaxpr/hqk,qhd->khd/dot_general | solution.py:139
  130.2 2.0 %convolution_convert_fusion.1 = bf16[1024,512]{1,0:T(8,128)(2,1)S(1)} fusion(bf16[1024,384]{1,0:T(8,128)(2,1)} %bitcast.201, bf16[512,128]{1,0:T(8,128)(2,1)} %param.22, bf16[512,128]{1,0:T(8,128)(2,1)} %param.21, bf16[512,128]{1,0:T(8,128)(2,1)} %param.20), kind=kOutput, calls=%fused_computation.56 | convolution fusion | flops 404357120 | bytes 2228224 | tf_op jit(solution)/shard_map/dot_general | solution.py:17
  133.6 20.4 %reduce-scatter.9.cloned.1.call-done = bf16[128,1024]{1,0:T(8,128)(2,1)} async-done(((bf16[512,1024]{1,0:T(8,128)(2,1)}), bf16[128,1024]{1,0:T(8,128)(2,1)}) %reduce-scatter.9.cloned.1.call-update) | async-done | bytes 262160
  154.0 1.8 copy.35
  155.8 5.5 %all-to-all-start.3 = ((bf16[8,128,128]{2,1,0:T(8,128)(2,1)}), bf16[8,128,128]{2,1,0:T(8,128)(2,1)S(1)}, u32[]{:S(2)}, u32[]{:S(2)}) async-start(bf16[8,128,128]{2,1,0:T(8,128)(2,1)} %bitcast.23), calls=%async_computation.3 | async-start | bytes 524288 | tf_op jit(solution)/shard_map/all_to_all | solution.py:173
  161.3 20.0 %reduce-scatter.7.cloned.1.call-done = bf16[128,1024]{1,0:T(8,128)(2,1)} async-done(((bf16[512,1024]{1,0:T(8,128)(2,1)}), bf16[128,1024]{1,0:T(8,128)(2,1)}) %reduce-scatter.7.cloned.1.call-update) | async-done | bytes 262160
  182.5 1.7 add_convert_fusion
  (135 shorter events, 36.8 us)
Async XLA Ops:
  7.2 37.9 %copy-start = (bf16[1024,512]{1,0:T(8,128)(2,1)S(1)}, bf16[1024,512]{1,0:T(8,128)(2,1)}, u32[]{:S(2)}) copy-start(bf16[1024,512]{1,0:T(8,128)(2,1)} %param.15) | copy-start | bytes 3145732
  7.2 50.8 %copy-start.17 = (s32[8,8]{1,0:T(8,128)S(1)}, s32[8,8]{1,0:T(8,128)}, u32[]{:S(2)}) copy-start(s32[8,8]{1,0:T(8,128)} %param.19) | copy-start | bytes 772
  7.2 50.8 %copy-start.14 = (s32[1,1024]{1,0:T(1,128)S(1)}, s32[1,1024]{1,0:T(1,128)}, u32[]{:S(2)}) copy-start(s32[1,1024]{1,0:T(1,128)} %param.14) | copy-start | bytes 12292
  11.4 32.7 %copy-start.15 = (s32[512,1]{0,1:T(1,128)}, s32[512,1]{0,1:T(1,128)S(1)}, u32[]{:S(2)}) copy-start(s32[512,1]{0,1:T(1,128)S(1)} %get-tuple-element.174) | copy-start | bytes 6148
  14.5 13.7 %all-to-all-start.1 = ((s32[8,128,1]{1,2,0:T(1,128)}), s32[8,128,1]{1,2,0:T(1,128)S(1)}, u32[]{:S(2)}, u32[]{:S(2)}) async-start(s32[8,128,1]{1,2,0:T(1,128)} %bitcast.18), calls=%async_computation.1 | async-start | bytes 8192 | tf_op jit(solution)/shard_map/all_to_all | solution.py:68
  39.5 27.6 %all-to-all-start = ((bf16[8,128,512]{2,1,0:T(8,128)(2,1)}), bf16[8,128,512]{2,1,0:T(8,128)(2,1)S(1)}, u32[]{:S(2)}, u32[]{:S(2)}) async-start(bf16[8,128,512]{2,1,0:T(8,128)(2,1)} %bitcast.186), calls=%async_computation | async-start | bytes 2097152 | tf_op jit(solution)/shard_map/all_to_all | solution.py:59
  43.1 32.4 %all-gather.2.cloned.1.call-start = ((), (), s32[]{:S(2)}) async-start(), calls=%async_computation.6 | async-start | bytes 1310720 | tf_op jit(solution)/shard_map/all_gather | solution.py:70
  45.1 30.4 %copy-start.5 = (bf16[512,256]{1,0:T(8,128)(2,1)}, bf16[512,256]{1,0:T(8,128)(2,1)S(1)}, u32[]{:S(2)}) copy-start(bf16[512,256]{1,0:T(8,128)(2,1)S(1)} %constant_dynamic-update-slice_fusion.1) | copy-start | bytes 786436
  46.4 28.2 %copy-start.13 = (bf16[128,512]{1,0:T(8,128)(2,1)S(1)}, bf16[128,512]{1,0:T(8,128)(2,1)}, u32[]{:S(2)}) copy-start(bf16[128,512]{1,0:T(8,128)(2,1)} %param.23) | copy-start | bytes 393220
  50.5 103.5 %reduce-scatter.9.cloned.1.call-start = ((), (), s32[]{:S(2)}) async-start(), calls=%async_computation.8 | async-start | bytes 1310720
  78.7 6.5 %copy-start.6 = (bf16[2,512,4,32]{1,3,2,0:T(8,128)(2,1)}, bf16[2,512,4,32]{1,3,2,0:T(8,128)(2,1)S(1)}, u32[]{:S(2)}) copy-start(bf16[2,512,4,32]{1,3,2,0:T(8,128)(2,1)S(1)} %get-tuple-element.315) | copy-start | bytes 786436 | tf_op jit(solution)/shard_map/while
  78.7 6.5 %copy-start.8 = (bf16[2,512,4,32]{1,3,2,0:T(8,128)(2,1)}, bf16[2,512,4,32]{1,3,2,0:T(8,128)(2,1)S(1)}, u32[]{:S(2)}) copy-start(bf16[2,512,4,32]{1,3,2,0:T(8,128)(2,1)S(1)} %get-tuple-element.318) | copy-start | bytes 786436 | tf_op jit(solution)/shard_map/while
  78.7 6.5 %copy-start.10 = (bf16[2,512,4,32]{1,3,2,0:T(8,128)(2,1)}, bf16[2,512,4,32]{1,3,2,0:T(8,128)(2,1)S(1)}, u32[]{:S(2)}) copy-start(bf16[2,512,4,32]{1,3,2,0:T(8,128)(2,1)S(1)} %get-tuple-element.316) | copy-start | bytes 786436 | tf_op jit(solution)/shard_map/while
  81.0 4.2 %copy-start.12 = (bf16[1024,4,32]{0,2,1:T(8,128)(2,1)S(1)}, bf16[1024,4,32]{0,2,1:T(8,128)(2,1)}, u32[]{:S(2)}) copy-start(bf16[1024,4,32]{0,2,1:T(8,128)(2,1)} %get-tuple-element.317) | copy-start | bytes 786436 | tf_op jit(solution)/shard_map/while
  82.6 6.1 %copy-start.1 = (f32[4,512,1024]{2,1,0:T(8,128)}, f32[4,512,1024]{2,1,0:T(8,128)S(1)}, u32[]{:S(2)}) copy-start(f32[4,512,1024]{2,1,0:T(8,128)S(1)} %get-tuple-element.271) | copy-start | bytes 25165828 | tf_op jit(solution)/shard_map/while
  95.7 5.7 %copy-start.3 = (bf16[4,512,1024]{2,1,0:T(8,128)(2,1)S(1)}, bf16[4,512,1024]{2,1,0:T(8,128)(2,1)}, u32[]{:S(2)}) copy-start(bf16[4,512,1024]{2,1,0:T(8,128)(2,1)} %copy-done.2) | copy-start | bytes 12582916 | tf_op jit(solution)/shard_map/while
  95.7 6.6 %copy-start.7 = (bf16[2,512,4,32]{1,3,2,0:T(8,128)(2,1)S(1)}, bf16[2,512,4,32]{1,3,2,0:T(8,128)(2,1)}, u32[]{:S(2)}) copy-start(bf16[2,512,4,32]{1,3,2,0:T(8,128)(2,1)} %copy-done.6) | copy-start | bytes 786436 | tf_op jit(solution)/shard_map/while
  95.7 6.6 %copy-start.9 = (bf16[2,512,4,32]{1,3,2,0:T(8,128)(2,1)S(1)}, bf16[2,512,4,32]{1,3,2,0:T(8,128)(2,1)}, u32[]{:S(2)}) copy-start(bf16[2,512,4,32]{1,3,2,0:T(8,128)(2,1)} %copy-done.8) | copy-start | bytes 786436 | tf_op jit(solution)/shard_map/while
  95.7 6.6 %copy-start.11 = (bf16[2,512,4,32]{1,3,2,0:T(8,128)(2,1)S(1)}, bf16[2,512,4,32]{1,3,2,0:T(8,128)(2,1)}, u32[]{:S(2)}) copy-start(bf16[2,512,4,32]{1,3,2,0:T(8,128)(2,1)} %copy-done.10) | copy-start | bytes 786436 | tf_op jit(solution)/shard_map/while
  102.3 6.5 %copy-start.6 = (bf16[2,512,4,32]{1,3,2,0:T(8,128)(2,1)}, bf16[2,512,4,32]{1,3,2,0:T(8,128)(2,1)S(1)}, u32[]{:S(2)}) copy-start(bf16[2,512,4,32]{1,3,2,0:T(8,128)(2,1)S(1)} %get-tuple-element.315) | copy-start | bytes 786436 | tf_op jit(solution)/shard_map/while
  102.3 6.5 %copy-start.8 = (bf16[2,512,4,32]{1,3,2,0:T(8,128)(2,1)}, bf16[2,512,4,32]{1,3,2,0:T(8,128)(2,1)S(1)}, u32[]{:S(2)}) copy-start(bf16[2,512,4,32]{1,3,2,0:T(8,128)(2,1)S(1)} %get-tuple-element.318) | copy-start | bytes 786436 | tf_op jit(solution)/shard_map/while
  102.4 6.5 %copy-start.10 = (bf16[2,512,4,32]{1,3,2,0:T(8,128)(2,1)}, bf16[2,512,4,32]{1,3,2,0:T(8,128)(2,1)S(1)}, u32[]{:S(2)}) copy-start(bf16[2,512,4,32]{1,3,2,0:T(8,128)(2,1)S(1)} %get-tuple-element.316) | copy-start | bytes 786436 | tf_op jit(solution)/shard_map/while
  104.8 4.2 %copy-start.12 = (bf16[1024,4,32]{0,2,1:T(8,128)(2,1)S(1)}, bf16[1024,4,32]{0,2,1:T(8,128)(2,1)}, u32[]{:S(2)}) copy-start(bf16[1024,4,32]{0,2,1:T(8,128)(2,1)} %get-tuple-element.317) | copy-start | bytes 786436 | tf_op jit(solution)/shard_map/while
  106.3 6.1 %copy-start.1 = (f32[4,512,1024]{2,1,0:T(8,128)}, f32[4,512,1024]{2,1,0:T(8,128)S(1)}, u32[]{:S(2)}) copy-start(f32[4,512,1024]{2,1,0:T(8,128)S(1)} %get-tuple-element.271) | copy-start | bytes 25165828 | tf_op jit(solution)/shard_map/while
  119.5 5.9 %copy-start.3 = (bf16[4,512,1024]{2,1,0:T(8,128)(2,1)S(1)}, bf16[4,512,1024]{2,1,0:T(8,128)(2,1)}, u32[]{:S(2)}) copy-start(bf16[4,512,1024]{2,1,0:T(8,128)(2,1)} %copy-done.2) | copy-start | bytes 12582916 | tf_op jit(solution)/shard_map/while
  119.5 6.7 %copy-start.7 = (bf16[2,512,4,32]{1,3,2,0:T(8,128)(2,1)S(1)}, bf16[2,512,4,32]{1,3,2,0:T(8,128)(2,1)}, u32[]{:S(2)}) copy-start(bf16[2,512,4,32]{1,3,2,0:T(8,128)(2,1)} %copy-done.6) | copy-start | bytes 786436 | tf_op jit(solution)/shard_map/while
  119.5 6.7 %copy-start.9 = (bf16[2,512,4,32]{1,3,2,0:T(8,128)(2,1)S(1)}, bf16[2,512,4,32]{1,3,2,0:T(8,128)(2,1)}, u32[]{:S(2)}) copy-start(bf16[2,512,4,32]{1,3,2,0:T(8,128)(2,1)} %copy-done.8) | copy-start | bytes 786436 | tf_op jit(solution)/shard_map/while
  119.5 6.7 %copy-start.11 = (bf16[2,512,4,32]{1,3,2,0:T(8,128)(2,1)S(1)}, bf16[2,512,4,32]{1,3,2,0:T(8,128)(2,1)}, u32[]{:S(2)}) copy-start(bf16[2,512,4,32]{1,3,2,0:T(8,128)(2,1)} %copy-done.10) | copy-start | bytes 786436 | tf_op jit(solution)/shard_map/while
  126.3 35.0 %copy-start.16 = (s32[512,1]{0,1:T(1,128)S(1)}, s32[512,1]{0,1:T(1,128)}, u32[]{:S(2)}) copy-start(s32[512,1]{0,1:T(1,128)} %copy-done.15) | copy-start | bytes 6148
  126.3 59.3 %copy-start.18 = (pred[512]{0:T(512)(128)(4,1)S(1)}, pred[512]{0:T(512)(128)(4,1)}, u32[]{:S(2)}) copy-start(pred[512]{0:T(512)(128)(4,1)} %get-tuple-element.173) | copy-start | bytes 1540
  130.2 51.2 %reduce-scatter.7.cloned.1.call-start = ((), (), s32[]{:S(2)}) async-start(), calls=%async_computation.7 | async-start | bytes 1310720
  155.8 28.4 %all-to-all-start.3 = ((bf16[8,128,128]{2,1,0:T(8,128)(2,1)}), bf16[8,128,128]{2,1,0:T(8,128)(2,1)S(1)}, u32[]{:S(2)}, u32[]{:S(2)}) async-start(bf16[8,128,128]{2,1,0:T(8,128)(2,1)} %bitcast.23), calls=%async_computation.3 | async-start | bytes 524288 | tf_op jit(solution)/shard_map/all_to_all | solution.py:173
  (3 other events, 4.9 us)
Sparse Core Ops, SparseCore 0:
  50.6 18.1 all-gather.1
  130.3 23.6 reduce-scatter.8
  156.5 24.7 reduce-scatter.6
where the time goes:
time: 194 us; the launch traced here: 193 us
  waiting for transfers between devices  53.3 us (27%)
  local copies, waits for them, and re-layouts  40.3 us (21%)
  matrix products  36.6 us (19%)
  other arithmetic  20.4 us (11%)
  starting transfers between devices  16.5 us (9%)
  between operations  14.1 us (7%)
  blocking collectives  11.3 us (6%)
    unnamed x5, waiting for transfers between devices  40.5 us
    dot_general x2, matrix products, attend(): jnp.einsum('hqk,qhd->khd', probabilities_low, gradient_block, preferred_e...  11.6 us
    all_to_all x1, blocking collectives, on_device(): lax.all_to_all(row_send, 'band', split_axis=0, concat_axis=0, tiled=True)  11.3 us
    unnamed x27, local copies, waits for them, and re-layouts  10.2 us
    all_to_all x1, waiting for transfers between devices, on_device(): lax.all_to_all(node_adjoint, 'band', split_axis=0, concat_axis=0, tiled=T...  8.53 us
    all_to_all x1, starting transfers between devices, on_device(): lax.all_to_all(cell_send, 'band', split_axis=0, concat_axis=0, tiled=True)  7.31 us
    dot_general x5, matrix products, dot_transposed(): lax.dot_general(left, right, (((1,), (1,)), ((), ())), preferred_element_...  6.76 us
    dot_general x2, matrix products, attend(): jnp.einsum('qhd,khd->hqk', gradient_block, value_heads, preferred_element...  6.59 us
  transfers between devices with their start and end apart: 6, of which 4 were waited for; matrix products, arithmetic and copies ran while one was open for 17% of the time, Pallas kernels for 0%

commit v1 on v0

--- a/solution.py
+++ b/solution.py
@@ -1,8 +1,11 @@
+import functools
 import math
 
 import jax
 import jax.numpy as jnp
 from jax import lax
+from jax.experimental import pallas as pl
+from jax.experimental.pallas import tpu as pltpu
 from jax.sharding import PartitionSpec as P
 
 HEAD_DIM = 32
@@ -31,7 +34,7 @@
     return target * capacity + rank_within
 
 
-def on_device(
+def on_device_plain(
     node_adjoint,
     band_map,
     latents,
@@ -175,9 +178,464 @@
     return (node_grad, observation_grad)
 
 
+TILE = 256
+HEADS_PER_PASS = 2
+MESH = pl.DeviceIdType.MESH
+
+
+def dot_first(left, right):
+    return lax.dot_general(
+        left, right, (((0,), (0,)), ((), ())), preferred_element_type=jnp.float32
+    )
+
+
+def column_of(row, rows=128):
+    wide = jnp.transpose(jnp.broadcast_to(row.astype(jnp.float32), (rows, row.shape[1])))
+    return wide[:, :1].astype(jnp.int32)
+
+
+def encoder_kernel(
+    bands,
+    models,
+    adjoint_ref,
+    map_ref,
+    latents_ref,
+    observed_ref,
+    band_ref,
+    cell_ref,
+    mask_ref,
+    wq_ref,
+    wk_ref,
+    wv_ref,
+    wo_ref,
+    node_out,
+    observed_out,
+    key_send,
+    value_send,
+    hot_send,
+    grad_send,
+    key_got,
+    value_got,
+    hot_got,
+    grad_got,
+    adj_got,
+    query_s,
+    query_t,
+    skey_s,
+    svalue_s,
+    grad_s,
+    grad_t,
+    key_heads,
+    value_heads,
+    bias_s,
+    dkey_t,
+    dvalue_t,
+    dquery_s,
+    dscore_s,
+    prob_s,
+    back_send,
+    back_got,
+    node_send,
+    node_got,
+    obs_send,
+    obs_got,
+    in_send,
+    in_recv,
+    back_send_sem,
+    back_recv_sem,
+    node_send_sem,
+    node_recv_sem,
+    obs_send_sem,
+    obs_recv_sem,
+):
+    me = lax.axis_index("band")
+    mine = lax.axis_index("mp")
+    nodes = latents_ref.shape[0]
+    columns = wq_ref.shape[1]
+    heads = columns // HEAD_DIM
+    observed = observed_ref.shape[0]
+    capacity = key_got.shape[1]
+    slots = bands * capacity
+    group = grad_got.shape[1]
+    blocks = mask_ref.shape[1]
+    tiles = nodes // TILE
+    per_tile = TILE // BLOCK
+    passes = heads // HEADS_PER_PASS
+    span = HEADS_PER_PASS * HEAD_DIM
+    factor = 1.0 / math.sqrt(HEAD_DIM)
+    low = jnp.bfloat16
+
+    def band_peer(off):
+        return lax.rem(me + off, bands)
+
+    def band_source(off):
+        return lax.rem(me + bands - off, bands)
+
+    def model_peer(off):
+        return lax.rem(mine + off, models)
+
+    barrier = pltpu.get_barrier_semaphore()
+    for off in range(1, bands):
+        pl.semaphore_signal(
+            barrier, inc=1, device_id={"band": band_peer(off)}, device_id_type=MESH
+        )
+    for off in range(1, models):
+        pl.semaphore_signal(
+            barrier, inc=1, device_id={"mp": model_peer(off)}, device_id_type=MESH
+        )
+
+    target = band_ref[...]
+    onehot = jnp.where(
+        lax.broadcasted_iota(jnp.int32, (bands, observed), 0) == target, 1.0, 0.0
+    )
+    before = jnp.where(
+        lax.broadcasted_iota(jnp.int32, (observed, observed), 0)
+        < lax.broadcasted_iota(jnp.int32, (observed, observed), 1),
+        1.0,
+        0.0,
+    ).astype(low)
+    earlier = dot_wide(onehot.astype(low), before)
+    rank = jnp.sum(earlier * onehot, axis=0, keepdims=True)
+    slot_row = target * capacity + rank.astype(jnp.int32)
+    place = jnp.where(
+        lax.broadcasted_iota(jnp.int32, (slots, observed), 0) == slot_row, 1.0, 0.0
+    ).astype(low)
+    keys_here = dot_wide(observed_ref[...], wk_ref[...]).astype(low)
+    key_send[...] = dot_wide(place, keys_here).astype(low).reshape(bands, capacity, columns)
+    cell_hot = jnp.where(
+        lax.broadcasted_iota(jnp.int32, (blocks, observed), 0) == (cell_ref[...] >> 7), 1.0, 0.0
+    ).astype(low)
+    cell_hot = jnp.concatenate([cell_hot, jnp.zeros((16 - blocks, observed), low)], axis=0)
+    hot = dot_transposed(cell_hot, place).astype(low)
+    for s in range(bands):
+        hot_send[s] = hot[:, s * capacity : (s + 1) * capacity]
+
+    def incoming(kind, off, source, landing):
+        return pltpu.make_async_remote_copy(
+            src_ref=source,
+            dst_ref=landing,
+            send_sem=in_send.at[kind, off],
+            recv_sem=in_recv.at[kind, off],
+            device_id={"band": band_peer(off)},
+            device_id_type=MESH,
+        )
+
+    def start_in(kind, source, landing):
+        for off in range(1, bands):
+            incoming(kind, off, source.at[band_peer(off)], landing.at[me]).start()
+
+    def wait_in(kind, source, landing):
+        for off in range(1, bands):
+            incoming(kind, off, source.at[band_peer(off)], landing.at[band_source(off)]).wait()
+
+    pl.semaphore_wait(barrier, bands + models - 2)
+    start_in(0, key_send, key_got)
+    start_in(1, hot_send, hot_got)
+    values_here = dot_wide(observed_ref[...], wv_ref[...]).astype(low)
+    value_send[...] = dot_wide(place, values_here).astype(low).reshape(bands, capacity, columns)
+    start_in(2, value_send, value_got)
+    grad_send[...] = (
+        dot_transposed(adjoint_ref[...], wo_ref[...]).astype(low).reshape(bands, group, columns)
+    )
+    start_in(3, grad_send, grad_got)
+
+    my_columns = pl.ds(pl.multiple_of(mine * columns, columns), columns)
+
+    def adjoint_rows(q):
+        return adjoint_ref.at[pl.ds(pl.multiple_of(q * group, group), group), my_columns]
+
+    for off in range(1, bands):
+        incoming(4, off, adjoint_rows(band_peer(off)), adj_got.at[me]).start()
+    key_got[me] = key_send[me]
+    hot_got[me] = hot_send[me]
+    value_got[me] = value_send[me]
+    grad_got[me] = grad_send[me]
+    adj_got[me] = adjoint_ref[pl.ds(pl.multiple_of(me * group, group), group), my_columns]
+
+    queries = (dot_wide(latents_ref[...], wq_ref[...]) * factor).astype(low)
+    query_s[...] = queries
+    turned = jnp.transpose(queries)
+    for t in range(tiles):
+        query_t[t] = turned[:, t * TILE : (t + 1) * TILE]
+    skey_s[...] = dot_wide(latents_ref[...], wk_ref[...]).astype(low)
+    svalue_s[...] = dot_wide(latents_ref[...], wv_ref[...]).astype(low)
+    dkey_t[...] = jnp.zeros_like(dkey_t)
+    dvalue_t[...] = jnp.zeros_like(dvalue_t)
+    lane_head = lax.broadcasted_iota(jnp.int32, (1, columns), 1) // HEAD_DIM
+
+    permute = jnp.where(
+        lax.broadcasted_iota(jnp.int32, (nodes, nodes), 1) == column_of(map_ref[...]), 1.0, 0.0
+    ).astype(low)
+    slot_column = column_of(slot_row)
+
+    def split_heads(landed, kept):
+        whole = landed[...].reshape(slots, columns)
+        for h in range(heads):
+            kept[h] = jnp.where(lane_head == h, whole.astype(jnp.float32), 0.0).astype(low)
+
+    wait_in(0, key_send, key_got)
+    split_heads(key_got, key_heads)
+    wait_in(1, hot_send, hot_got)
+    hot_all = jnp.concatenate([hot_got[s] for s in range(bands)], axis=1)
+    mask = jnp.concatenate(
+        [mask_ref[...].astype(jnp.float32), jnp.zeros((blocks, 16 - blocks), jnp.float32)], axis=1
+    ).astype(low)
+    bias = jnp.where(dot_wide(mask, hot_all) > 0.5, 0.0, -1e30)
+    for b in range(blocks):
+        bias_s[b] = bias[b : b + 1, :]
+    wait_in(2, value_send, value_got)
+    split_heads(value_got, value_heads)
+    wait_in(3, grad_send, grad_got)
+    grads = dot_wide(permute, grad_got[...].reshape(nodes, columns)).astype(low)
+    grad_s[...] = grads
+    turned = jnp.transpose(grads)
+    for t in range(tiles):
+        grad_t[t] = turned[:, t * TILE : (t + 1) * TILE]
+
+    def back(part, which, off, source_band, landing_band):
+        rows = pl.ds(which * columns + part * span, span)
+        return pltpu.make_async_remote_copy(
+            src_ref=back_send.at[source_band, rows],
+            dst_ref=back_got.at[landing_band, rows],
+            send_sem=back_send_sem.at[part * 2 + which, off],
+            recv_sem=back_recv_sem.at[part * 2 + which, off],
+            device_id={"band": band_peer(off)},
+            device_id_type=MESH,
+        )
+
+    def node_copy(off, t):
+        return pltpu.make_async_remote_copy(
+            src_ref=node_send.at[model_peer(off), t],
+            dst_ref=node_got.at[off - 1, t],
+            send_sem=node_send_sem.at[off - 1, t],
+            recv_sem=node_recv_sem.at[off - 1, t],
+            device_id={"mp": model_peer(off)},
+            device_id_type=MESH,
+        )
+
+    for part in range(passes):
+
+        def tile_step(t, carry, part=part):
+            rows = pl.ds(pl.multiple_of(t * TILE, TILE), TILE)
+            query = query_s[rows, :]
+            grad = grad_s[rows, :]
+            query_wide = query.astype(jnp.float32)
+            grad_wide = grad.astype(jnp.float32)
+            skey_wide = skey_s[rows, :].astype(jnp.float32)
+            svalue_wide = svalue_s[rows, :].astype(jnp.float32)
+            own_products = query_wide * skey_wide
+            own_dproducts = grad_wide * svalue_wide
+            penalty = bias_s[pl.ds(t * per_tile, per_tile)]
+            if part == 0:
+                dquery = jnp.zeros((TILE, columns), jnp.float32)
+                own_dscores = jnp.zeros((TILE, columns), jnp.float32)
+                own_probs = jnp.zeros((TILE, columns), jnp.float32)
+            else:
+                dquery = dquery_s[rows, :]
+                own_dscores = dscore_s[rows, :]
+                own_probs = prob_s[rows, :]
+            for h in range(part * HEADS_PER_PASS, (part + 1) * HEADS_PER_PASS):
+                lanes = lane_head == h
+                keys = key_heads[h]
+                scores = dot_transposed(query, keys)
+                scores = (scores.reshape(per_tile, BLOCK, slots) + penalty).reshape(TILE, slots)
+                own_score = jnp.sum(jnp.where(lanes, own_products, 0.0), axis=1, keepdims=True)
+                own_dprob = jnp.sum(jnp.where(lanes, own_dproducts, 0.0), axis=1, keepdims=True)
+                highest = jnp.maximum(jnp.max(scores, axis=1, keepdims=True), own_score)
+                weights = jnp.exp(scores - highest)
+                own_weight = jnp.exp(own_score - highest)
+                inverse = 1.0 / (jnp.sum(weights, axis=1, keepdims=True) + own_weight)
+                probs = weights * inverse
+                own_prob = own_weight * inverse
+                dprobs = dot_transposed(grad, value_heads[h])
+                centre = jnp.sum(probs * dprobs, axis=1, keepdims=True) + own_prob * own_dprob
+                dscore_low = (probs * (dprobs - centre)).astype(low)
+                probs_low = probs.astype(low)
+                own_dscore = own_prob * (own_dprob - centre)
+                dquery = dquery + dot_wide(dscore_low, keys)
+                own_dscores = jnp.where(lanes, own_dscore, own_dscores)
+                own_probs = jnp.where(lanes, own_prob, own_probs)
+                features = pl.ds(h * HEAD_DIM, HEAD_DIM)
+                dkey_t[features, :] += dot_wide(query_t[t, features, :], dscore_low)
+                dvalue_t[features, :] += dot_wide(grad_t[t, features, :], probs_low)
+            if part < passes - 1:
+                dquery_s[rows, :] = dquery
+                dscore_s[rows, :] = own_dscores
+                prob_s[rows, :] = own_probs
+            else:
+                pieces = jnp.concatenate(
+                    [
+                        ((dquery + own_dscores * skey_wide) * factor).astype(low),
+                        (own_dscores * query_wide).astype(low),
+                        (own_probs * grad_wide).astype(low),
+                    ],
+                    axis=1,
+                )
+                weights_all = jnp.concatenate([wq_ref[...], wk_ref[...], wv_ref[...]], axis=1)
+                term = dot_transposed(pieces, weights_all).astype(low)
+                for j in range(models):
+                    node_send[j, t] = term[:, j * columns : (j + 1) * columns]
+                for off in range(1, models):
+                    node_copy(off, t).start()
+            return carry
+
+        lax.fori_loop(0, tiles, tile_step, 0)
+        for which, total in ((0, dkey_t), (1, dvalue_t)):
+            done = total[pl.ds(part * span, span), :].astype(low)
+            for s in range(bands):
+                back_send[s, pl.ds(which * columns + part * span, span), :] = done[
+                    :, s * capacity : (s + 1) * capacity
+                ]
+            for off in range(1, bands):
+                back(part, which, off, band_peer(off), me).start()
+    back_got[me] = back_send[me]
+
+    for off in range(1, bands):
+        incoming(4, off, adjoint_rows(band_peer(off)), adj_got.at[band_source(off)]).wait()
+    adjoint_mine = dot_wide(permute, adj_got[...].reshape(nodes, columns))
+    gather = jnp.where(
+        lax.broadcasted_iota(jnp.int32, (observed, slots), 1) == slot_column, 1.0, 0.0
+    ).astype(low)
+    for part in range(passes):
+        for which in range(2):
+            for off in range(1, bands):
+                back(part, which, off, band_peer(off), band_source(off)).wait()
+    returned = jnp.concatenate([back_got[s] for s in range(bands)], axis=1)
+    own_pairs = dot_transposed(gather, returned).astype(low)
+    w_pair = jnp.concatenate([wk_ref[...], wv_ref[...]], axis=1)
+    obs_term = dot_transposed(own_pairs, w_pair).astype(low)
+    for j in range(models):
+        obs_send[j] = obs_term[:, j * columns : (j + 1) * columns]
+
+    def obs_copy(off):
+        return pltpu.make_async_remote_copy(
+            src_ref=obs_send.at[model_peer(off)],
+            dst_ref=obs_got.at[off - 1],
+            send_sem=obs_send_sem.at[off - 1],
+            recv_sem=obs_recv_sem.at[off - 1],
+            device_id={"mp": model_peer(off)},
+            device_id_type=MESH,
+        )
+
+    for off in range(1, models):
+        obs_copy(off).start()
+    for t in range(tiles):
+        for off in range(1, models):
+            node_copy(off, t).wait()
+        rows = slice(t * TILE, (t + 1) * TILE)
+        total = node_send[mine, t].astype(jnp.float32)
+        for off in range(1, models):
+            total = total + node_got[off - 1, t].astype(jnp.float32)
+        node_out[rows, :] = (adjoint_mine[rows, :] + total).astype(low)
+    total = obs_send[mine].astype(jnp.float32)
+    for off in range(1, models):
+        obs_copy(off).wait()
+        total = total + obs_got[off - 1].astype(jnp.float32)
+    observed_out[...] = total.astype(low)
+
+
+def on_device(
+    node_adjoint,
+    band_map,
+    latents,
+    observations,
+    route_band,
+    route_cell,
+    block_mask,
+    w_query,
+    w_key,
+    w_value,
+    w_out,
+):
+    bands = lax.axis_size("band")
+    models = lax.axis_size("mp")
+    nodes = latents.shape[0]
+    columns = w_query.shape[1]
+    heads = columns // HEAD_DIM
+    observed = observations.shape[0]
+    capacity = 2 * observed // bands
+    slots = capacity * bands
+    group = nodes // bands
+    blocks = block_mask.shape[1]
+    tiles = nodes // TILE
+    passes = heads // HEADS_PER_PASS
+    low, wide = jnp.bfloat16, jnp.float32
+    dma = pltpu.SemaphoreType.DMA
+    vmem = pl.BlockSpec(memory_space=pltpu.VMEM)
+    return pl.pallas_call(
+        functools.partial(encoder_kernel, bands, models),
+        out_shape=(
+            jax.ShapeDtypeStruct((nodes, columns), low),
+            jax.ShapeDtypeStruct((observed, columns), low),
+        ),
+        in_specs=[vmem] * 11,
+        out_specs=(vmem, vmem),
+        scratch_shapes=[
+            pltpu.VMEM((bands, capacity, columns), low),
+            pltpu.VMEM((bands, capacity, columns), low),
+            pltpu.VMEM((bands, 16, capacity), low),
+            pltpu.VMEM((bands, group, columns), low),
+            pltpu.VMEM((bands, capacity, columns), low),
+            pltpu.VMEM((bands, capacity, columns), low),
+            pltpu.VMEM((bands, 16, capacity), low),
+            pltpu.VMEM((bands, group, columns), low),
+            pltpu.VMEM((bands, group, columns), low),
+            pltpu.VMEM((nodes, columns), low),
+            pltpu.VMEM((tiles, columns, TILE), low),
+            pltpu.VMEM((nodes, columns), low),
+            pltpu.VMEM((nodes, columns), low),
+            pltpu.VMEM((nodes, columns), low),
+            pltpu.VMEM((tiles, columns, TILE), low),
+            pltpu.VMEM((heads, slots, columns), low),
+            pltpu.VMEM((heads, slots, columns), low),
+            pltpu.VMEM((blocks, 1, slots), wide),
+            pltpu.VMEM((columns, slots), wide),
+            pltpu.VMEM((columns, slots), wide),
+            pltpu.VMEM((nodes, columns), wide),
+            pltpu.VMEM((nodes, columns), wide),
+            pltpu.VMEM((nodes, columns), wide),
+            pltpu.VMEM((bands, 2 * columns, capacity), low),
+            pltpu.VMEM((bands, 2 * columns, capacity), low),
+            pltpu.VMEM((models, tiles, TILE, columns), low),
+            pltpu.VMEM((models - 1, tiles, TILE, columns), low),
+            pltpu.VMEM((models, observed, columns), low),
+            pltpu.VMEM((models - 1, observed, columns), low),
+            dma((5, bands)),
+            dma((5, bands)),
+            dma((2 * passes, bands)),
+            dma((2 * passes, bands)),
+            dma((models - 1, tiles)),
+            dma((models - 1, tiles)),
+            dma((models - 1,)),
+            dma((models - 1,)),
+        ],
+        compiler_params=pltpu.CompilerParams(collective_id=0, has_side_effects=True),
+    )(
+        node_adjoint,
+        band_map,
+        latents,
+        observations,
+        route_band.reshape(1, observed),
+        route_cell.reshape(1, observed),
+        block_mask,
+        w_query,
+        w_key,
+        w_value,
+        w_out,
+    )
+
+
 def solution(mesh):
+    bands = mesh.shape["band"]
+
+    def body(*arrays):
+        capacity = 2 * arrays[3].shape[0] // bands
+        group = arrays[0].shape[0] // bands
+        tiled = capacity % 128 == 0 and group % 16 == 0
+        return (on_device if tiled else on_device_plain)(*arrays)
+
     return jax.shard_map(
-        on_device,
+        body,
         mesh=mesh,
         in_specs=(
             P("band", None),

time: 194 us -> 67.3 us (0.35)
  Pallas kernels: 0 us -> 63.4 us
  waiting for transfers between devices: 53.3 us -> 0 us
  local copies, waits for them, and re-layouts: 40.3 us -> 2.36 us
  matrix products: 36.6 us -> 0 us
  other arithmetic: 20.4 us -> 0 us
  starting transfers between devices: 16.5 us -> 0 us
  between operations: 14.1 us -> 0.65 us
  blocking collectives: 11.3 us -> 0 us
    pallas_call x0 -> x1, Pallas kernels: none -> 63.4 us  [on_device(): pl.pallas_call(functools.partial(encoder_kernel, bands, models), out_shap...]
    unnamed x5 -> x0, waiting for transfers between devices: 40.5 us -> none
    dot_general x18 -> x0, matrix products: 36.6 us -> none  [the longest x2 11.6 us: attend(): jnp.einsum('hqk,qhd->khd', probabilities_low, gradient_block, preferred_e...]
    all_to_all x3 -> x0, starting transfers between devices: 16.4 us -> none  [the longest x1 7.31 us: on_device(): lax.all_to_all(cell_send, 'band', split_axis=0, concat_axis=0, tiled=True)]
    all_to_all x3 -> x0, waiting for transfers between devices: 12.8 us -> none  [the longest x1 8.53 us: on_device(): lax.all_to_all(node_adjoint, 'band', split_axis=0, concat_axis=0, tiled=T...]
    all_to_all x1 -> x0, blocking collectives: 11.3 us -> none  [on_device(): lax.all_to_all(row_send, 'band', split_axis=0, concat_axis=0, tiled=True)]
    convert_element_type x11 -> x0, other arithmetic: 9.05 us -> none  [the longest x2 5.33 us: attend(): score_gradient_narrow = dscore.astype(jnp.bfloat16)]
    unnamed x27 -> x4, local copies, waits for them, and re-layouts: 10.2 us -> 2.36 us
  transfers between devices with their start and end apart: 6 -> 0, of which waited for: 4 -> 0; matrix products, arithmetic and copies ran while one was open for 17% -> 0% of each run, Pallas kernels for 0% -> 0%
where the time goes in v1:
time: 67.3 us; the launch traced here: 66.4 us
  Pallas kernels  63.4 us (94%)
  local copies, waits for them, and re-layouts  2.36 us (4%)
    pallas_call x1, Pallas kernels, on_device(): pl.pallas_call(functools.partial(encoder_kernel, bands, models), out_shap...  63.4 us
    unnamed x4, local copies, waits for them, and re-layouts  2.36 us

profile of v1, /device:TPU:0, one launch (start us, length us, event | category | flops | bytes accessed | tf_op | source)
XLA Modules:
  0.0 66.4 jit_solution(17840885514668204165)
XLA Ops:
  0.6 63.4 %shard_map.122 = (bf16[1024,128]{1,0:T(8,128)(2,1)}, bf16[512,128]{1,0:T(8,128)(2,1)}) custom-call(bf16[1024,512]{1,0:T(8,128)(2,1)} %adjoint_ref.1, s32[1,1024]{1,0:T(1,128)} %map_ref.1, bf16[1024,512]{1,0:T(8,128)(2,1)} %latents_ref.1, bf16[512,512]{1,0:T(8,128)(2,1)} %observed_ref.1, s32[1,512]{1,0:T(1,128)} %bitcast.2, s32[1,512]{1,0:T(1,128)} %bitcast.3, ...), custom_call_target="tpu_custom_call" | custom-call | tf_op jit(solution)/shard_map/pallas_call | solution.py:565
  64.1 0.0 copy-start
  64.1 1.7 %copy.15 = bf16[1024,128]{1,0:T(8,128)(2,1)} copy(bf16[1024,128]{1,0:T(8,128)(2,1)} %get-tuple-element.4) | data formatting | bytes 524288
  65.8 0.0 copy-done
  65.8 0.7 copy.16
Async XLA Ops:
  64.1 1.7 %copy-start = (bf16[512,128]{1,0:T(8,128)(2,1)S(1)}, bf16[512,128]{1,0:T(8,128)(2,1)}, u32[]{:S(2)}) copy-start(bf16[512,128]{1,0:T(8,128)(2,1)} %get-tuple-element.5) | copy-start | bytes 393220

commit v2 on v1

--- a/solution.py
+++ b/solution.py
@@ -179,7 +179,8 @@
 
 
 TILE = 256
-HEADS_PER_PASS = 2
+HEADS_PER_PASS = 1
+UNROLL = 2
 MESH = pl.DeviceIdType.MESH
 
 
@@ -210,12 +211,10 @@
     wo_ref,
     node_out,
     observed_out,
-    key_send,
-    value_send,
+    row_send,
     hot_send,
     grad_send,
-    key_got,
-    value_got,
+    row_got,
     hot_got,
     grad_got,
     adj_got,
@@ -236,17 +235,23 @@
     back_send,
     back_got,
     node_send,
+    node_pair,
+    node_sum,
     node_got,
     obs_send,
+    obs_pair,
+    obs_sum,
     obs_got,
     in_send,
     in_recv,
+    row_send_sem,
+    row_recv_sem,
     back_send_sem,
     back_recv_sem,
     node_send_sem,
     node_recv_sem,
-    obs_send_sem,
-    obs_recv_sem,
+    pair_send_sem,
+    pair_recv_sem,
 ):
     me = lax.axis_index("band")
     mine = lax.axis_index("mp")
@@ -254,7 +259,7 @@
     columns = wq_ref.shape[1]
     heads = columns // HEAD_DIM
     observed = observed_ref.shape[0]
-    capacity = key_got.shape[1]
+    capacity = row_got.shape[2]
     slots = bands * capacity
     group = grad_got.shape[1]
     blocks = mask_ref.shape[1]
@@ -273,6 +278,18 @@
 
     def model_peer(off):
         return lax.rem(mine + off, models)
+
+    def model_source(off):
+        return lax.rem(mine + models - off, models)
+
+    chips = models // 2
+    side = lax.rem(mine, 2)
+    chip = mine // 2
+    partner = mine + 1 - 2 * side
+    my_columns = pl.ds(pl.multiple_of(mine * columns, columns), columns)
+
+    def chip_peer(off):
+        return lax.rem(chip + off, chips)
 
     barrier = pltpu.get_barrier_semaphore()
     for off in range(1, bands):
@@ -300,8 +317,9 @@
     place = jnp.where(
         lax.broadcasted_iota(jnp.int32, (slots, observed), 0) == slot_row, 1.0, 0.0
     ).astype(low)
-    keys_here = dot_wide(observed_ref[...], wk_ref[...]).astype(low)
-    key_send[...] = dot_wide(place, keys_here).astype(low).reshape(bands, capacity, columns)
+    row_send[...] = (
+        dot_wide(place, observed_ref[:, my_columns]).astype(low).reshape(bands, capacity, columns)
+    )
     cell_hot = jnp.where(
         lax.broadcasted_iota(jnp.int32, (blocks, observed), 0) == (cell_ref[...] >> 7), 1.0, 0.0
     ).astype(low)
@@ -328,39 +346,57 @@
         for off in range(1, bands):
             incoming(kind, off, source.at[band_peer(off)], landing.at[band_source(off)]).wait()
 
+    def arrived(off):
+        return incoming(0, off, row_send.at[band_peer(off)], row_got.at[mine, band_source(off)])
+
+    def forward(off, hop, owner):
+        block = row_got.at[owner, band_source(off)]
+        return pltpu.make_async_remote_copy(
+            src_ref=block,
+            dst_ref=block,
+            send_sem=row_send_sem.at[hop - 1, off],
+            recv_sem=row_recv_sem.at[hop - 1, off],
+            device_id={"mp": model_peer(hop)},
+            device_id_type=MESH,
+        )
+
+    def adjoint_rows(q):
+        return adjoint_ref.at[pl.ds(pl.multiple_of(q * group, group), group), my_columns]
+
+    row_got[mine, me] = row_send[me]
     pl.semaphore_wait(barrier, bands + models - 2)
-    start_in(0, key_send, key_got)
+    start_in(0, row_send, row_got.at[mine])
     start_in(1, hot_send, hot_got)
-    values_here = dot_wide(observed_ref[...], wv_ref[...]).astype(low)
-    value_send[...] = dot_wide(place, values_here).astype(low).reshape(bands, capacity, columns)
-    start_in(2, value_send, value_got)
+    for hop in range(1, models):
+        forward(0, hop, mine).start()
     grad_send[...] = (
         dot_transposed(adjoint_ref[...], wo_ref[...]).astype(low).reshape(bands, group, columns)
     )
-    start_in(3, grad_send, grad_got)
-
-    my_columns = pl.ds(pl.multiple_of(mine * columns, columns), columns)
-
-    def adjoint_rows(q):
-        return adjoint_ref.at[pl.ds(pl.multiple_of(q * group, group), group), my_columns]
-
+    start_in(2, grad_send, grad_got)
     for off in range(1, bands):
-        incoming(4, off, adjoint_rows(band_peer(off)), adj_got.at[me]).start()
-    key_got[me] = key_send[me]
+        incoming(3, off, adjoint_rows(band_peer(off)), adj_got.at[me]).start()
+
+    def pass_on(off):
+        arrived(off).wait_recv()
+        for hop in range(1, models):
+            forward(off, hop, mine).start()
+
     hot_got[me] = hot_send[me]
-    value_got[me] = value_send[me]
     grad_got[me] = grad_send[me]
     adj_got[me] = adjoint_ref[pl.ds(pl.multiple_of(me * group, group), group), my_columns]
-
     queries = (dot_wide(latents_ref[...], wq_ref[...]) * factor).astype(low)
     query_s[...] = queries
     turned = jnp.transpose(queries)
     for t in range(tiles):
         query_t[t] = turned[:, t * TILE : (t + 1) * TILE]
+    for off in range(1, bands // 2):
+        pass_on(off)
     skey_s[...] = dot_wide(latents_ref[...], wk_ref[...]).astype(low)
     svalue_s[...] = dot_wide(latents_ref[...], wv_ref[...]).astype(low)
     dkey_t[...] = jnp.zeros_like(dkey_t)
     dvalue_t[...] = jnp.zeros_like(dvalue_t)
+    for off in range(bands // 2, bands):
+        pass_on(off)
     lane_head = lax.broadcasted_iota(jnp.int32, (1, columns), 1) // HEAD_DIM
 
     permute = jnp.where(
@@ -368,13 +404,16 @@
     ).astype(low)
     slot_column = column_of(slot_row)
 
-    def split_heads(landed, kept):
-        whole = landed[...].reshape(slots, columns)
+    def split_heads(weights, kept):
+        whole = jnp.zeros((slots, columns), jnp.float32)
+        for j in range(models):
+            whole = whole + dot_wide(
+                row_got[j].reshape(slots, columns), weights[j * columns : (j + 1) * columns, :]
+            )
+        whole = whole.astype(low).astype(jnp.float32)
         for h in range(heads):
-            kept[h] = jnp.where(lane_head == h, whole.astype(jnp.float32), 0.0).astype(low)
-
-    wait_in(0, key_send, key_got)
-    split_heads(key_got, key_heads)
+            kept[h] = jnp.where(lane_head == h, whole, 0.0).astype(low)
+
     wait_in(1, hot_send, hot_got)
     hot_all = jnp.concatenate([hot_got[s] for s in range(bands)], axis=1)
     mask = jnp.concatenate(
@@ -383,9 +422,12 @@
     bias = jnp.where(dot_wide(mask, hot_all) > 0.5, 0.0, -1e30)
     for b in range(blocks):
         bias_s[b] = bias[b : b + 1, :]
-    wait_in(2, value_send, value_got)
-    split_heads(value_got, value_heads)
-    wait_in(3, grad_send, grad_got)
+    for off in range(bands):
+        for hop in range(1, models):
+            forward(off, hop, model_source(hop)).wait_recv()
+    split_heads(wk_ref, key_heads)
+    split_heads(wv_ref, value_heads)
+    wait_in(2, grad_send, grad_got)
     grads = dot_wide(permute, grad_got[...].reshape(nodes, columns)).astype(low)
     grad_s[...] = grads
     turned = jnp.transpose(grads)
@@ -403,19 +445,50 @@
             device_id_type=MESH,
         )
 
-    def node_copy(off, t):
+    def pair_copy(source, landing, index):
         return pltpu.make_async_remote_copy(
-            src_ref=node_send.at[model_peer(off), t],
-            dst_ref=node_got.at[off - 1, t],
-            send_sem=node_send_sem.at[off - 1, t],
-            recv_sem=node_recv_sem.at[off - 1, t],
-            device_id={"mp": model_peer(off)},
+            src_ref=source,
+            dst_ref=landing,
+            send_sem=pair_send_sem.at[index],
+            recv_sem=pair_recv_sem.at[index],
+            device_id={"mp": partner},
             device_id_type=MESH,
         )
 
+    def cross_copy(off, source, landing, index):
+        return pltpu.make_async_remote_copy(
+            src_ref=source,
+            dst_ref=landing,
+            send_sem=node_send_sem.at[off - 1, index],
+            recv_sem=node_recv_sem.at[off - 1, index],
+            device_id={"mp": chip_peer(off) * 2 + side},
+            device_id_type=MESH,
+        )
+
+    def node_exchange(t):
+        return pair_copy(node_send.at[1 - side, t], node_pair.at[t], t)
+
+    def node_cross(off, t):
+        return cross_copy(off, node_sum.at[off - 1, t], node_got.at[off - 1, t], t)
+
+    def obs_exchange():
+        return pair_copy(obs_send.at[1 - side], obs_pair, tiles)
+
+    def obs_cross(off):
+        return cross_copy(off, obs_sum.at[off - 1], obs_got.at[off - 1], tiles)
+
+    def node_reduce(t):
+        node_exchange(t).wait()
+        for off in range(1, chips):
+            c = chip_peer(off)
+            node_sum[off - 1, t] = (
+                node_send[side, t, c].astype(jnp.float32) + node_pair[t, c].astype(jnp.float32)
+            ).astype(low)
+            node_cross(off, t).start()
+
     for part in range(passes):
 
-        def tile_step(t, carry, part=part):
+        def tile_step(t, part=part):
             rows = pl.ds(pl.multiple_of(t * TILE, TILE), TILE)
             query = query_s[rows, :]
             grad = grad_s[rows, :]
@@ -474,12 +547,22 @@
                 weights_all = jnp.concatenate([wq_ref[...], wk_ref[...], wv_ref[...]], axis=1)
                 term = dot_transposed(pieces, weights_all).astype(low)
                 for j in range(models):
-                    node_send[j, t] = term[:, j * columns : (j + 1) * columns]
-                for off in range(1, models):
-                    node_copy(off, t).start()
-            return carry
-
-        lax.fori_loop(0, tiles, tile_step, 0)
+                    node_send[j % 2, t, j // 2] = term[:, j * columns : (j + 1) * columns]
+                node_exchange(t).start()
+
+        if part < passes - 1:
+
+            def some_tiles(i, carry):
+                for u in range(UNROLL):
+                    tile_step(i * UNROLL + u)
+                return carry
+
+            lax.fori_loop(0, tiles // UNROLL, some_tiles, 0)
+        else:
+            for t in range(tiles):
+                tile_step(t)
+                if t >= UNROLL:
+                    node_reduce(t - UNROLL)
         for which, total in ((0, dkey_t), (1, dvalue_t)):
             done = total[pl.ds(part * span, span), :].astype(low)
             for s in range(bands):
@@ -489,9 +572,11 @@
             for off in range(1, bands):
                 back(part, which, off, band_peer(off), me).start()
     back_got[me] = back_send[me]
+    for t in range(tiles - UNROLL, tiles):
+        node_reduce(t)
 
     for off in range(1, bands):
-        incoming(4, off, adjoint_rows(band_peer(off)), adj_got.at[band_source(off)]).wait()
+        incoming(3, off, adjoint_rows(band_peer(off)), adj_got.at[band_source(off)]).wait()
     adjoint_mine = dot_wide(permute, adj_got[...].reshape(nodes, columns))
     gather = jnp.where(
         lax.broadcasted_iota(jnp.int32, (observed, slots), 1) == slot_column, 1.0, 0.0
@@ -505,31 +590,31 @@
     w_pair = jnp.concatenate([wk_ref[...], wv_ref[...]], axis=1)
     obs_term = dot_transposed(own_pairs, w_pair).astype(low)
     for j in range(models):
-        obs_send[j] = obs_term[:, j * columns : (j + 1) * columns]
-
-    def obs_copy(off):
-        return pltpu.make_async_remote_copy(
-            src_ref=obs_send.at[model_peer(off)],
-            dst_ref=obs_got.at[off - 1],
-            send_sem=obs_send_sem.at[off - 1],
-            recv_sem=obs_recv_sem.at[off - 1],
-            device_id={"mp": model_peer(off)},
-            device_id_type=MESH,
-        )
-
-    for off in range(1, models):
-        obs_copy(off).start()
+        obs_send[j % 2, j // 2] = obs_term[:, j * columns : (j + 1) * columns]
+    obs_exchange().start()
+    obs_exchange().wait()
+    for off in range(1, chips):
+        c = chip_peer(off)
+        obs_sum[off - 1] = (
+            obs_send[side, c].astype(jnp.float32) + obs_pair[c].astype(jnp.float32)
+        ).astype(low)
+        obs_cross(off).start()
     for t in range(tiles):
-        for off in range(1, models):
-            node_copy(off, t).wait()
         rows = slice(t * TILE, (t + 1) * TILE)
-        total = node_send[mine, t].astype(jnp.float32)
-        for off in range(1, models):
+        total = node_send[side, t, chip].astype(jnp.float32)
+        total = total + node_pair[t, chip].astype(jnp.float32)
+        for off in range(1, chips):
+            node_cross(off, t).wait()
             total = total + node_got[off - 1, t].astype(jnp.float32)
         node_out[rows, :] = (adjoint_mine[rows, :] + total).astype(low)
-    total = obs_send[mine].astype(jnp.float32)
-    for off in range(1, models):
-        obs_copy(off).wait()
+    for off in range(1, bands):
+        arrived(off).wait_send()
+    for off in range(bands):
+        for hop in range(1, models):
+            forward(off, hop, mine).wait_send()
+    total = obs_send[side, chip].astype(jnp.float32) + obs_pair[chip].astype(jnp.float32)
+    for off in range(1, chips):
+        obs_cross(off).wait()
         total = total + obs_got[off - 1].astype(jnp.float32)
     observed_out[...] = total.astype(low)
 
@@ -549,6 +634,7 @@
 ):
     bands = lax.axis_size("band")
     models = lax.axis_size("mp")
+    chips = models // 2
     nodes = latents.shape[0]
     columns = w_query.shape[1]
     heads = columns // HEAD_DIM
@@ -572,11 +658,9 @@
         out_specs=(vmem, vmem),
         scratch_shapes=[
             pltpu.VMEM((bands, capacity, columns), low),
-            pltpu.VMEM((bands, capacity, columns), low),
             pltpu.VMEM((bands, 16, capacity), low),
             pltpu.VMEM((bands, group, columns), low),
-            pltpu.VMEM((bands, capacity, columns), low),
-            pltpu.VMEM((bands, capacity, columns), low),
+            pltpu.VMEM((models, bands, capacity, columns), low),
             pltpu.VMEM((bands, 16, capacity), low),
             pltpu.VMEM((bands, group, columns), low),
             pltpu.VMEM((bands, group, columns), low),
@@ -596,18 +680,24 @@
             pltpu.VMEM((nodes, columns), wide),
             pltpu.VMEM((bands, 2 * columns, capacity), low),
             pltpu.VMEM((bands, 2 * columns, capacity), low),
-            pltpu.VMEM((models, tiles, TILE, columns), low),
-            pltpu.VMEM((models - 1, tiles, TILE, columns), low),
-            pltpu.VMEM((models, observed, columns), low),
-            pltpu.VMEM((models - 1, observed, columns), low),
-            dma((5, bands)),
-            dma((5, bands)),
+            pltpu.VMEM((2, tiles, chips, TILE, columns), low),
+            pltpu.VMEM((tiles, chips, TILE, columns), low),
+            pltpu.VMEM((chips - 1, tiles, TILE, columns), low),
+            pltpu.VMEM((chips - 1, tiles, TILE, columns), low),
+            pltpu.VMEM((2, chips, observed, columns), low),
+            pltpu.VMEM((chips, observed, columns), low),
+            pltpu.VMEM((chips - 1, observed, columns), low),
+            pltpu.VMEM((chips - 1, observed, columns), low),
+            dma((4, bands)),
+            dma((4, bands)),
+            dma((models - 1, bands)),
+            dma((models - 1, bands)),
             dma((2 * passes, bands)),
             dma((2 * passes, bands)),
-            dma((models - 1, tiles)),
-            dma((models - 1, tiles)),
-            dma((models - 1,)),
-            dma((models - 1,)),
+            dma((chips - 1, tiles + 1)),
+            dma((chips - 1, tiles + 1)),
+            dma((tiles + 1,)),
+            dma((tiles + 1,)),
         ],
         compiler_params=pltpu.CompilerParams(collective_id=0, has_side_effects=True),
     )(

time: 67.3 us -> 63.8 us (0.948); the launches traced: 66.4 us -> 63.7 us
  Pallas kernels: 63.4 us -> 60.7 us
    pallas_call x1, Pallas kernels: 63.4 us -> 60.7 us  [on_device(): pl.pallas_call(functools.partial(encoder_kernel, bands, models), out_shap...]
where the time goes in v2:
time: 63.8 us; the launch traced here: 63.7 us
  Pallas kernels  60.7 us (95%)
  local copies, waits for them, and re-layouts  2.36 us (4%)
  between operations  0.65 us (1%)
    pallas_call x1, Pallas kernels, on_device(): pl.pallas_call(functools.partial(encoder_kernel, bands, models), out_shap...  60.7 us
    unnamed x4, local copies, waits for them, and re-layouts  2.36 us

profile of v2, /device:TPU:0, one launch (start us, length us, event | category | flops | bytes accessed | tf_op | source)
XLA Modules:
  0.0 63.7 jit_solution(17690776802719161493)
XLA Ops:
  0.6 60.7 %shard_map.122 = (bf16[1024,128]{1,0:T(8,128)(2,1)}, bf16[512,128]{1,0:T(8,128)(2,1)}) custom-call(bf16[1024,512]{1,0:T(8,128)(2,1)} %adjoint_ref.1, s32[1,1024]{1,0:T(1,128)} %map_ref.1, bf16[1024,512]{1,0:T(8,128)(2,1)} %latents_ref.1, bf16[512,512]{1,0:T(8,128)(2,1)} %observed_ref.1, s32[1,512]{1,0:T(1,128)} %bitcast.2, s32[1,512]{1,0:T(1,128)} %bitcast.3, ...), custom_call_target="tpu_custom_call" | custom-call | tf_op jit(solution)/shard_map/pallas_call | solution.py:651
  61.3 0.0 copy-start
  61.3 1.7 %copy.15 = bf16[1024,128]{1,0:T(8,128)(2,1)} copy(bf16[1024,128]{1,0:T(8,128)(2,1)} %get-tuple-element.4) | data formatting | bytes 524288
  63.0 0.0 copy-done
  63.0 0.7 %copy.16 = bf16[512,128]{1,0:T(8,128)(2,1)} copy(bf16[512,128]{1,0:T(8,128)(2,1)S(1)} %copy-done) | data formatting | bytes 262144
Async XLA Ops:
  61.3 1.7 %copy-start = (bf16[512,128]{1,0:T(8,128)(2,1)S(1)}, bf16[512,128]{1,0:T(8,128)(2,1)}, u32[]{:S(2)}) copy-start(bf16[512,128]{1,0:T(8,128)(2,1)} %get-tuple-element.5) | copy-start | bytes 393220

commit v3 on v2

--- a/solution.py
+++ b/solution.py
@@ -198,19 +198,27 @@
 def encoder_kernel(
     bands,
     models,
-    adjoint_ref,
+    adjoint_hbm,
     map_ref,
-    latents_ref,
-    observed_ref,
+    latents_hbm,
+    observed_hbm,
     band_ref,
     cell_ref,
     mask_ref,
+    wq_hbm,
+    wk_hbm,
+    wv_hbm,
+    wo_hbm,
+    node_out,
+    observed_out,
+    adjoint_ref,
+    latents_ref,
+    observed_ref,
     wq_ref,
     wk_ref,
     wv_ref,
     wo_ref,
-    node_out,
-    observed_out,
+    load_sem,
     row_send,
     hot_send,
     grad_send,
@@ -229,9 +237,12 @@
     bias_s,
     dkey_t,
     dvalue_t,
-    dquery_s,
+    dscore_low_s,
     dscore_s,
     prob_s,
+    permute_s,
+    gather_s,
+    own_s,
     back_send,
     back_got,
     node_send,
@@ -291,6 +302,20 @@
     def chip_peer(off):
         return lax.rem(chip + off, chips)
 
+    loads = {}
+    for index, (name, source, landing) in enumerate(
+        (
+            ("observed", observed_hbm, observed_ref),
+            ("adjoint", adjoint_hbm, adjoint_ref),
+            ("wo", wo_hbm, wo_ref),
+            ("latents", latents_hbm, latents_ref),
+            ("wq", wq_hbm, wq_ref),
+            ("wk", wk_hbm, wk_ref),
+            ("wv", wv_hbm, wv_ref),
+        )
+    ):
+        loads[name] = pltpu.make_async_copy(source, landing, load_sem.at[index])
+
     barrier = pltpu.get_barrier_semaphore()
     for off in range(1, bands):
         pl.semaphore_signal(
@@ -301,6 +326,8 @@
             barrier, inc=1, device_id={"mp": model_peer(off)}, device_id_type=MESH
         )
 
+    for copy in loads.values():
+        copy.start()
     target = band_ref[...]
     onehot = jnp.where(
         lax.broadcasted_iota(jnp.int32, (bands, observed), 0) == target, 1.0, 0.0
@@ -317,6 +344,7 @@
     place = jnp.where(
         lax.broadcasted_iota(jnp.int32, (slots, observed), 0) == slot_row, 1.0, 0.0
     ).astype(low)
+    loads["observed"].wait()
     row_send[...] = (
         dot_wide(place, observed_ref[:, my_columns]).astype(low).reshape(bands, capacity, columns)
     )
@@ -364,14 +392,38 @@
         return adjoint_ref.at[pl.ds(pl.multiple_of(q * group, group), group), my_columns]
 
     row_got[mine, me] = row_send[me]
+    loads["adjoint"].wait()
+    loads["wo"].wait()
+    grad_send[...] = (
+        dot_transposed(adjoint_ref[...], wo_ref[...]).astype(low).reshape(bands, group, columns)
+    )
+    hot_got[me] = hot_send[me]
+    grad_got[me] = grad_send[me]
+    adj_got[me] = adjoint_ref[pl.ds(pl.multiple_of(me * group, group), group), my_columns]
+    for name in ("latents", "wq", "wk", "wv"):
+        loads[name].wait()
+    queries = (dot_wide(latents_ref[...], wq_ref[...]) * factor).astype(low)
+    query_s[...] = queries
+    turned = jnp.transpose(queries)
+    for t in range(tiles):
+        query_t[t] = turned[:, t * TILE : (t + 1) * TILE]
+    skey_s[...] = dot_wide(latents_ref[...], wk_ref[...]).astype(low)
+    svalue_s[...] = dot_wide(latents_ref[...], wv_ref[...]).astype(low)
+    dkey_t[...] = jnp.zeros_like(dkey_t)
+    dvalue_t[...] = jnp.zeros_like(dvalue_t)
+    lane_head = lax.broadcasted_iota(jnp.int32, (1, columns), 1) // HEAD_DIM
+    permute_s[...] = jnp.where(
+        lax.broadcasted_iota(jnp.int32, (nodes, nodes), 1) == column_of(map_ref[...]), 1.0, 0.0
+    ).astype(low)
+    gather_s[...] = jnp.where(
+        lax.broadcasted_iota(jnp.int32, (observed, slots), 1) == column_of(slot_row), 1.0, 0.0
+    ).astype(low)
+    own_s[...] = query_s[...].astype(jnp.float32) * skey_s[...].astype(jnp.float32)
     pl.semaphore_wait(barrier, bands + models - 2)
     start_in(0, row_send, row_got.at[mine])
     start_in(1, hot_send, hot_got)
     for hop in range(1, models):
         forward(0, hop, mine).start()
-    grad_send[...] = (
-        dot_transposed(adjoint_ref[...], wo_ref[...]).astype(low).reshape(bands, group, columns)
-    )
     start_in(2, grad_send, grad_got)
     for off in range(1, bands):
         incoming(3, off, adjoint_rows(band_peer(off)), adj_got.at[me]).start()
@@ -381,28 +433,8 @@
         for hop in range(1, models):
             forward(off, hop, mine).start()
 
-    hot_got[me] = hot_send[me]
-    grad_got[me] = grad_send[me]
-    adj_got[me] = adjoint_ref[pl.ds(pl.multiple_of(me * group, group), group), my_columns]
-    queries = (dot_wide(latents_ref[...], wq_ref[...]) * factor).astype(low)
-    query_s[...] = queries
-    turned = jnp.transpose(queries)
-    for t in range(tiles):
-        query_t[t] = turned[:, t * TILE : (t + 1) * TILE]
-    for off in range(1, bands // 2):
+    for off in range(1, bands):
         pass_on(off)
-    skey_s[...] = dot_wide(latents_ref[...], wk_ref[...]).astype(low)
-    svalue_s[...] = dot_wide(latents_ref[...], wv_ref[...]).astype(low)
-    dkey_t[...] = jnp.zeros_like(dkey_t)
-    dvalue_t[...] = jnp.zeros_like(dvalue_t)
-    for off in range(bands // 2, bands):
-        pass_on(off)
-    lane_head = lax.broadcasted_iota(jnp.int32, (1, columns), 1) // HEAD_DIM
-
-    permute = jnp.where(
-        lax.broadcasted_iota(jnp.int32, (nodes, nodes), 1) == column_of(map_ref[...]), 1.0, 0.0
-    ).astype(low)
-    slot_column = column_of(slot_row)
 
     def split_heads(weights, kept):
         whole = jnp.zeros((slots, columns), jnp.float32)
@@ -428,7 +460,7 @@
     split_heads(wk_ref, key_heads)
     split_heads(wv_ref, value_heads)
     wait_in(2, grad_send, grad_got)
-    grads = dot_wide(permute, grad_got[...].reshape(nodes, columns)).astype(low)
+    grads = dot_wide(permute_s[...], grad_got[...].reshape(nodes, columns)).astype(low)
     grad_s[...] = grads
     turned = jnp.transpose(grads)
     for t in range(tiles):
@@ -492,19 +524,15 @@
             rows = pl.ds(pl.multiple_of(t * TILE, TILE), TILE)
             query = query_s[rows, :]
             grad = grad_s[rows, :]
-            query_wide = query.astype(jnp.float32)
             grad_wide = grad.astype(jnp.float32)
-            skey_wide = skey_s[rows, :].astype(jnp.float32)
             svalue_wide = svalue_s[rows, :].astype(jnp.float32)
-            own_products = query_wide * skey_wide
+            own_products = own_s[rows, :]
             own_dproducts = grad_wide * svalue_wide
             penalty = bias_s[pl.ds(t * per_tile, per_tile)]
             if part == 0:
-                dquery = jnp.zeros((TILE, columns), jnp.float32)
                 own_dscores = jnp.zeros((TILE, columns), jnp.float32)
                 own_probs = jnp.zeros((TILE, columns), jnp.float32)
             else:
-                dquery = dquery_s[rows, :]
                 own_dscores = dscore_s[rows, :]
                 own_probs = prob_s[rows, :]
             for h in range(part * HEADS_PER_PASS, (part + 1) * HEADS_PER_PASS):
@@ -525,44 +553,21 @@
                 dscore_low = (probs * (dprobs - centre)).astype(low)
                 probs_low = probs.astype(low)
                 own_dscore = own_prob * (own_dprob - centre)
-                dquery = dquery + dot_wide(dscore_low, keys)
+                dscore_low_s[h, rows, :] = dscore_low
                 own_dscores = jnp.where(lanes, own_dscore, own_dscores)
                 own_probs = jnp.where(lanes, own_prob, own_probs)
                 features = pl.ds(h * HEAD_DIM, HEAD_DIM)
                 dkey_t[features, :] += dot_wide(query_t[t, features, :], dscore_low)
                 dvalue_t[features, :] += dot_wide(grad_t[t, features, :], probs_low)
-            if part < passes - 1:
-                dquery_s[rows, :] = dquery
-                dscore_s[rows, :] = own_dscores
-                prob_s[rows, :] = own_probs
-            else:
-                pieces = jnp.concatenate(
-                    [
-                        ((dquery + own_dscores * skey_wide) * factor).astype(low),
-                        (own_dscores * query_wide).astype(low),
-                        (own_probs * grad_wide).astype(low),
-                    ],
-                    axis=1,
-                )
-                weights_all = jnp.concatenate([wq_ref[...], wk_ref[...], wv_ref[...]], axis=1)
-                term = dot_transposed(pieces, weights_all).astype(low)
-                for j in range(models):
-                    node_send[j % 2, t, j // 2] = term[:, j * columns : (j + 1) * columns]
-                node_exchange(t).start()
-
-        if part < passes - 1:
-
-            def some_tiles(i, carry):
-                for u in range(UNROLL):
-                    tile_step(i * UNROLL + u)
-                return carry
-
-            lax.fori_loop(0, tiles // UNROLL, some_tiles, 0)
-        else:
-            for t in range(tiles):
-                tile_step(t)
-                if t >= UNROLL:
-                    node_reduce(t - UNROLL)
+            dscore_s[rows, :] = own_dscores
+            prob_s[rows, :] = own_probs
+
+        def some_tiles(i, carry):
+            for u in range(UNROLL):
+                tile_step(i * UNROLL + u)
+            return carry
+
+        lax.fori_loop(0, tiles // UNROLL, some_tiles, 0)
         for which, total in ((0, dkey_t), (1, dvalue_t)):
             done = total[pl.ds(part * span, span), :].astype(low)
             for s in range(bands):
@@ -572,21 +577,38 @@
             for off in range(1, bands):
                 back(part, which, off, band_peer(off), me).start()
     back_got[me] = back_send[me]
-    for t in range(tiles - UNROLL, tiles):
-        node_reduce(t)
-
+
+    weights_all = jnp.concatenate([wq_ref[...], wk_ref[...], wv_ref[...]], axis=1)
+    for t in range(tiles):
+        rows = slice(t * TILE, (t + 1) * TILE)
+        dquery = dot_wide(dscore_low_s[0, rows, :], key_heads[0])
+        for h in range(1, heads):
+            dquery = dquery + dot_wide(dscore_low_s[h, rows, :], key_heads[h])
+        own_dscores = dscore_s[rows, :]
+        pieces = jnp.concatenate(
+            [
+                ((dquery + own_dscores * skey_s[rows, :].astype(jnp.float32)) * factor).astype(low),
+                (own_dscores * query_s[rows, :].astype(jnp.float32)).astype(low),
+                (prob_s[rows, :] * grad_s[rows, :].astype(jnp.float32)).astype(low),
+            ],
+            axis=1,
+        )
+        term = dot_transposed(pieces, weights_all).astype(low)
+        for j in range(models):
+            node_send[j % 2, t, j // 2] = term[:, j * columns : (j + 1) * columns]
+        node_exchange(t).start()
+        if t:
+            node_reduce(t - 1)
     for off in range(1, bands):
         incoming(3, off, adjoint_rows(band_peer(off)), adj_got.at[band_source(off)]).wait()
-    adjoint_mine = dot_wide(permute, adj_got[...].reshape(nodes, columns))
-    gather = jnp.where(
-        lax.broadcasted_iota(jnp.int32, (observed, slots), 1) == slot_column, 1.0, 0.0
-    ).astype(low)
+    adjoint_mine = dot_wide(permute_s[...], adj_got[...].reshape(nodes, columns))
+    node_reduce(tiles - 1)
     for part in range(passes):
         for which in range(2):
             for off in range(1, bands):
                 back(part, which, off, band_peer(off), band_source(off)).wait()
     returned = jnp.concatenate([back_got[s] for s in range(bands)], axis=1)
-    own_pairs = dot_transposed(gather, returned).astype(low)
+    own_pairs = dot_transposed(gather_s[...], returned).astype(low)
     w_pair = jnp.concatenate([wk_ref[...], wv_ref[...]], axis=1)
     obs_term = dot_transposed(own_pairs, w_pair).astype(low)
     for j in range(models):
@@ -619,6 +641,11 @@
     observed_out[...] = total.astype(low)
 
 
+def write_kernel(node_ref, observed_ref, node_out, observed_out):
+    node_out[...] = node_ref[...]
+    observed_out[...] = observed_ref[...]
+
+
 def on_device(
     node_adjoint,
     band_map,
@@ -648,15 +675,24 @@
     low, wide = jnp.bfloat16, jnp.float32
     dma = pltpu.SemaphoreType.DMA
     vmem = pl.BlockSpec(memory_space=pltpu.VMEM)
-    return pl.pallas_call(
+    far = pl.BlockSpec(memory_space=pl.ANY)
+    grads = pl.pallas_call(
         functools.partial(encoder_kernel, bands, models),
         out_shape=(
             jax.ShapeDtypeStruct((nodes, columns), low),
             jax.ShapeDtypeStruct((observed, columns), low),
         ),
-        in_specs=[vmem] * 11,
+        in_specs=[far, vmem, far, far, vmem, vmem, vmem, far, far, far, far],
         out_specs=(vmem, vmem),
         scratch_shapes=[
+            pltpu.VMEM(node_adjoint.shape, low),
+            pltpu.VMEM(latents.shape, low),
+            pltpu.VMEM(observations.shape, low),
+            pltpu.VMEM(w_query.shape, low),
+            pltpu.VMEM(w_key.shape, low),
+            pltpu.VMEM(w_value.shape, low),
+            pltpu.VMEM(w_out.shape, low),
+            dma((7,)),
             pltpu.VMEM((bands, capacity, columns), low),
             pltpu.VMEM((bands, 16, capacity), low),
             pltpu.VMEM((bands, group, columns), low),
@@ -675,8 +711,11 @@
             pltpu.VMEM((blocks, 1, slots), wide),
             pltpu.VMEM((columns, slots), wide),
             pltpu.VMEM((columns, slots), wide),
+            pltpu.VMEM((heads, nodes, slots), low),
             pltpu.VMEM((nodes, columns), wide),
             pltpu.VMEM((nodes, columns), wide),
+            pltpu.VMEM((nodes, nodes), low),
+            pltpu.VMEM((observed, slots), low),
             pltpu.VMEM((nodes, columns), wide),
             pltpu.VMEM((bands, 2 * columns, capacity), low),
             pltpu.VMEM((bands, 2 * columns, capacity), low),
@@ -713,6 +752,12 @@
         w_value,
         w_out,
     )
+    return pl.pallas_call(
+        write_kernel,
+        out_shape=tuple(jax.ShapeDtypeStruct(g.shape, g.dtype) for g in grads),
+        in_specs=(vmem, vmem),
+        out_specs=(vmem, vmem),
+    )(*grads)
 
 
 def solution(mesh):

time: 63.8 us -> 59.6 us (0.934)
  local copies, waits for them, and re-layouts: 2.36 us -> 0 us
  Pallas kernels: 60.7 us -> 58.8 us
    pallas_call x1, Pallas kernels: 60.7 us -> 57.1 us  [on_device(): pl.pallas_call(functools.partial(encoder_kernel, bands, models), out_shap...]
    unnamed x4 -> x0, local copies, waits for them, and re-layouts: 2.36 us -> none
    pallas_call x0 -> x1, Pallas kernels: none -> 1.74 us  [on_device(): pl.pallas_call(write_kernel, out_shape=tuple((jax.ShapeDtypeStruct(g.shap...]
where the time goes in v3:
time: 59.6 us; the launch traced here: 59.4 us
  Pallas kernels  58.8 us (99%)
  between operations  0.64 us (1%)
    pallas_call x1, Pallas kernels, on_device(): pl.pallas_call(functools.partial(encoder_kernel, bands, models), out_shap...  57.1 us
    pallas_call x1, Pallas kernels, on_device(): pl.pallas_call(write_kernel, out_shape=tuple((jax.ShapeDtypeStruct(g.shap...  1.74 us

profile of v3, /device:TPU:0, one launch (start us, length us, event | category | flops | bytes accessed | tf_op | source)
XLA Modules:
  0.0 59.4 jit_solution(16343243294437630411)
XLA Ops:
  0.6 57.1 %shard_map.122 = (bf16[1024,128]{1,0:T(8,128)(2,1)}, bf16[512,128]{1,0:T(8,128)(2,1)}) custom-call(bf16[1024,512]{1,0:T(8,128)(2,1)} %adjoint_hbm.1, s32[1,1024]{1,0:T(1,128)} %map_ref.1, bf16[1024,512]{1,0:T(8,128)(2,1)} %latents_hbm.1, bf16[512,512]{1,0:T(8,128)(2,1)} %observed_hbm.1, s32[1,512]{1,0:T(1,128)} %bitcast.2, s32[1,512]{1,0:T(1,128)} %bitcast.3, ...), custom_call_target="tpu_custom_call" | custom-call | tf_op jit(solution)/shard_map/pallas_call | solution.py:679
  57.7 1.7 %shard_map.123 = (bf16[1024,128]{1,0:T(8,128)(2,1)}, bf16[512,128]{1,0:T(8,128)(2,1)}) custom-call(bf16[1024,128]{1,0:T(8,128)(2,1)} %get-tuple-element.4.node_ref, bf16[512,128]{1,0:T(8,128)(2,1)} %get-tuple-element.5.observed_ref), custom_call_target="tpu_custom_call" | custom-call | tf_op jit(solution)/shard_map/pallas_call | solution.py:755

commit v4 on v3

--- a/solution.py
+++ b/solution.py
@@ -400,25 +400,6 @@
     hot_got[me] = hot_send[me]
     grad_got[me] = grad_send[me]
     adj_got[me] = adjoint_ref[pl.ds(pl.multiple_of(me * group, group), group), my_columns]
-    for name in ("latents", "wq", "wk", "wv"):
-        loads[name].wait()
-    queries = (dot_wide(latents_ref[...], wq_ref[...]) * factor).astype(low)
-    query_s[...] = queries
-    turned = jnp.transpose(queries)
-    for t in range(tiles):
-        query_t[t] = turned[:, t * TILE : (t + 1) * TILE]
-    skey_s[...] = dot_wide(latents_ref[...], wk_ref[...]).astype(low)
-    svalue_s[...] = dot_wide(latents_ref[...], wv_ref[...]).astype(low)
-    dkey_t[...] = jnp.zeros_like(dkey_t)
-    dvalue_t[...] = jnp.zeros_like(dvalue_t)
-    lane_head = lax.broadcasted_iota(jnp.int32, (1, columns), 1) // HEAD_DIM
-    permute_s[...] = jnp.where(
-        lax.broadcasted_iota(jnp.int32, (nodes, nodes), 1) == column_of(map_ref[...]), 1.0, 0.0
-    ).astype(low)
-    gather_s[...] = jnp.where(
-        lax.broadcasted_iota(jnp.int32, (observed, slots), 1) == column_of(slot_row), 1.0, 0.0
-    ).astype(low)
-    own_s[...] = query_s[...].astype(jnp.float32) * skey_s[...].astype(jnp.float32)
     pl.semaphore_wait(barrier, bands + models - 2)
     start_in(0, row_send, row_got.at[mine])
     start_in(1, hot_send, hot_got)
@@ -433,8 +414,29 @@
         for hop in range(1, models):
             forward(off, hop, mine).start()
 
-    for off in range(1, bands):
+    for name in ("latents", "wq", "wk", "wv"):
+        loads[name].wait()
+    queries = (dot_wide(latents_ref[...], wq_ref[...]) * factor).astype(low)
+    query_s[...] = queries
+    turned = jnp.transpose(queries)
+    for t in range(tiles):
+        query_t[t] = turned[:, t * TILE : (t + 1) * TILE]
+    for off in range(1, bands // 2):
         pass_on(off)
+    skey_s[...] = dot_wide(latents_ref[...], wk_ref[...]).astype(low)
+    svalue_s[...] = dot_wide(latents_ref[...], wv_ref[...]).astype(low)
+    dkey_t[...] = jnp.zeros_like(dkey_t)
+    dvalue_t[...] = jnp.zeros_like(dvalue_t)
+    lane_head = lax.broadcasted_iota(jnp.int32, (1, columns), 1) // HEAD_DIM
+    for off in range(bands // 2, bands):
+        pass_on(off)
+    permute_s[...] = jnp.where(
+        lax.broadcasted_iota(jnp.int32, (nodes, nodes), 1) == column_of(map_ref[...]), 1.0, 0.0
+    ).astype(low)
+    gather_s[...] = jnp.where(
+        lax.broadcasted_iota(jnp.int32, (observed, slots), 1) == column_of(slot_row), 1.0, 0.0
+    ).astype(low)
+    own_s[...] = query_s[...].astype(jnp.float32) * skey_s[...].astype(jnp.float32)
 
     def split_heads(weights, kept):
         whole = jnp.zeros((slots, columns), jnp.float32)

time: 59.6 us -> 58.8 us (0.987)
  Pallas kernels: 58.8 us -> 57.9 us
    pallas_call x1, Pallas kernels: 57.1 us -> 56.2 us  [on_device(): pl.pallas_call(functools.partial(encoder_kernel, bands, models), out_shap...]
where the time goes in v4:
time: 58.8 us; the launch traced here: 58.6 us
  Pallas kernels  57.9 us (98%)
  between operations  0.64 us (1%)
    pallas_call x1, Pallas kernels, on_device(): pl.pallas_call(functools.partial(encoder_kernel, bands, models), out_shap...  56.2 us
    pallas_call x1, Pallas kernels, on_device(): pl.pallas_call(write_kernel, out_shape=tuple((jax.ShapeDtypeStruct(g.shap...  1.74 us

profile of v4, /device:TPU:0, one launch (start us, length us, event | category | flops | bytes accessed | tf_op | source)
XLA Modules:
  0.0 58.6 jit_solution(14447694728734629338)
XLA Ops:
  0.6 56.2 %shard_map.122 = (bf16[1024,128]{1,0:T(8,128)(2,1)}, bf16[512,128]{1,0:T(8,128)(2,1)}) custom-call(bf16[1024,512]{1,0:T(8,128)(2,1)} %adjoint_hbm.1, s32[1,1024]{1,0:T(1,128)} %map_ref.1, bf16[1024,512]{1,0:T(8,128)(2,1)} %latents_hbm.1, bf16[512,512]{1,0:T(8,128)(2,1)} %observed_hbm.1, s32[1,512]{1,0:T(1,128)} %bitcast.2, s32[1,512]{1,0:T(1,128)} %bitcast.3, ...), custom_call_target="tpu_custom_call" | custom-call | tf_op jit(solution)/shard_map/pallas_call | solution.py:681
  56.8 1.7 %shard_map.123 = (bf16[1024,128]{1,0:T(8,128)(2,1)}, bf16[512,128]{1,0:T(8,128)(2,1)}) custom-call(bf16[1024,128]{1,0:T(8,128)(2,1)} %get-tuple-element.4.node_ref, bf16[512,128]{1,0:T(8,128)(2,1)} %get-tuple-element.5.observed_ref), custom_call_target="tpu_custom_call" | custom-call | tf_op jit(solution)/shard_map/pallas_call | solution.py:757
